TPU v7x, 256 devices: a whole 4x4x8 slice. The times are simulated.
256 devices in a mesh: tm: 16 (over z, core), space: 16 (over y, x).
Axes of the slice: x: 4, y: 4, z: 8, core: 2. Of those that a mesh axis runs over, the one named last changes fastest.
Arguments:
- queries: bfloat16 [16, 2048, 48, 128], P('tm', 'space'), may hold values from -14 to 14
- noisy_keys: bfloat16 [16, 2048, 48, 128], P('tm', 'space'), may hold values from -14 to 14
- noisy_values: bfloat16 [16, 2048, 48, 128], P('tm', 'space'), may hold values from -6 to 6
- cache_keys: bfloat16 [16, 2048, 48, 128], P('tm', 'space'), may hold values from -12 to 12
- cache_values: bfloat16 [16, 2048, 48, 128], P('tm', 'space'), may hold values from -6 to 6
- block_list: int32 [16, 16, 12], P('tm'), may hold values from 0 to 63, as said below
- block_count: int32 [16, 16], P('tm'), may hold values from 1 to 12
- valid_tokens: int32 [16], replicated, may hold values from 1921 to 2048
Outputs:
- attended: bfloat16 [16, 2048, 48, 128], P('tm', 'space')
Inputs may be any that keep to these rules, and one draw needn't show every extreme that they name: `block_list`: entries index the 64 key blocks of stretch c's window in order of offset, the last 16 being stretch c's own blocks. The first block_count[c, a] entries are distinct and name only blocks of stretches 0 or later; the first of them is query block a's own block; later entries repeat that own block.
All inputs are finite; a program needn't handle non-finite values.
Results may differ from a plain program's by a relative error of at most 0.0035.
Values may be sent and summed in bfloat16 or wider, within the bound.
No kernel may reach another device: no remote copies, remote signals or barrier semaphores. Data moves between devices by JAX's collectives and lax.ppermute only.
A program may use at most 128 MiB of HBM per device.

v0:
```python
import math

import jax
import jax.numpy as jnp
from jax import lax
from jax.sharding import PartitionSpec as P

BLOCK = 128
WIN = 4
LIST = 12


NEG = -1e30


def passed_along(block, axis, distance):
    devices = range(lax.axis_size(axis))
    route = [(i - distance, i) for i in devices if i - distance in devices]
    return lax.ppermute(block, axis, route)


def hand_forward(pair):
    earlier = []
    carried = pair
    for distance in range(1, WIN):
        carried = passed_along(carried, "tm", 1)
        earlier.append(carried)
    return earlier


def on_device(
    queries,
    noisy_keys,
    noisy_values,
    cache_keys,
    cache_values,
    block_list,
    block_count,
    valid_tokens,
):
    stretch_now = lax.axis_index("tm")
    fresh = jnp.concatenate((queries, noisy_keys, noisy_values), 0)
    fresh = lax.all_to_all(fresh, "space", split_axis=2, concat_axis=1, tiled=True)
    own_cache = jnp.concatenate((cache_keys, cache_values), 0)
    earlier = hand_forward(own_cache)
    stacked = jnp.stack(earlier[::-1], 0)
    past = lax.all_to_all(stacked, "space", split_axis=3, concat_axis=2, tiled=True)
    stretch_len = fresh.shape[1]
    local_heads = fresh.shape[2]
    head_size = fresh.shape[3]
    block_total = stretch_len // BLOCK
    fresh_heads = jnp.transpose(fresh, (0, 2, 1, 3))
    past_heads = jnp.transpose(past, (1, 3, 0, 2, 4))
    window_keys = jnp.concatenate((past_heads[0], fresh_heads[1][:, None]), 1)
    window_values = jnp.concatenate((past_heads[1], fresh_heads[2][:, None]), 1)
    query_blocks = fresh_heads[0].reshape(local_heads, block_total, BLOCK, head_size)
    key_blocks = window_keys.reshape(local_heads, WIN * block_total, BLOCK, head_size)
    value_blocks = window_values.reshape(local_heads, WIN * block_total, BLOCK, head_size)
    positions = jnp.arange(stretch_len)
    sources = stretch_now - (WIN - 1) + jnp.arange(WIN)
    lengths = valid_tokens[jnp.clip(sources, 0, valid_tokens.shape[0] - 1)]
    key_live = ((sources[:, None] >= 0) & (positions[None, :] < lengths[:, None])).reshape(
        WIN * block_total, BLOCK
    )
    stretch_lists = block_list[0]
    stretch_counts = block_count[0]
    score_scale = 1.0 / math.sqrt(head_size)
    start_best = jnp.full((local_heads, block_total, BLOCK), NEG, jnp.float32)
    start_total = jnp.zeros((local_heads, block_total, BLOCK), jnp.float32)
    start_accum = jnp.zeros((local_heads, block_total, BLOCK, head_size), jnp.float32)

    def slot_step(slot_index, carry):
        row_best, row_total, accum = carry
        chosen = lax.dynamic_slice_in_dim(stretch_lists, slot_index, 1, 1)[:, 0]
        keys_here = key_blocks[:, chosen]
        values_here = value_blocks[:, chosen]
        scores = (
            jnp.einsum(
                "haqd,hakd->haqk", query_blocks, keys_here, preferred_element_type=jnp.float32
            )
            * score_scale
        )
        allowed = (slot_index < stretch_counts)[None, :, None, None] & key_live[chosen][
            None, :, None, :
        ]
        scores = jnp.where(allowed, scores, NEG)
        new_best = jnp.maximum(row_best, jnp.max(scores, axis=-1))
        weights = jnp.where(allowed, jnp.exp(scores - new_best[..., None]), 0.0)
        shrink = jnp.exp(row_best - new_best)
        row_total = row_total * shrink + jnp.sum(weights, axis=-1)
        pieces = jnp.einsum(
            "haqk,hakd->haqd",
            weights.astype(jnp.bfloat16),
            values_here,
            preferred_element_type=jnp.float32,
        )
        accum = accum * shrink[..., None] + pieces
        return (new_best, row_total, accum)

    row_best, row_total, accum = lax.fori_loop(
        0, LIST, slot_step, (start_best, start_total, start_accum)
    )
    mixed_rows = accum / row_total[..., None]
    mixed_rows = mixed_rows.reshape(local_heads, stretch_len, head_size)
    query_live = positions < valid_tokens[stretch_now]
    masked = jnp.where(query_live[None, :, None], mixed_rows, 0.0).astype(jnp.bfloat16)
    attended_local = jnp.transpose(masked, (1, 0, 2))
    return lax.all_to_all(attended_local[None], "space", split_axis=1, concat_axis=2, tiled=True)


def solution(mesh):
    placed = (
        P("tm", "space", None, None),
        P("tm", "space", None, None),
        P("tm", "space", None, None),
        P("tm", "space", None, None),
        P("tm", "space", None, None),
        P("tm", None, None),
        P("tm", None),
        P(),
    )
    return jax.shard_map(
        on_device,
        mesh=mesh,
        in_specs=placed,
        out_specs=P("tm", "space", None, None),
        check_vma=False,
    )
```

profile of v0, /device:TPU:192, one launch (start us, length us, event | category | flops | bytes accessed | tf_op | source)
XLA Modules:
  0.0 597.0 jit_solution(18413690183494990930)
XLA Ops:
  4.9 36.7 %collective-permute-done = bf16[2,128,48,128]{3,1,0,2:T(8,128)(2,1)S(1)} collective-permute-done((bf16[2,128,48,128]{3,1,0,2:T(8,128)(2,1)S(1)}, bf16[2,128,48,128]{3,1,0,2:T(8,128)(2,1)S(1)}, u32[]{:S(2)}, u32[]{:S(2)}) %collective-permute-start) | collective-permute-done | bytes 3145760 | tf_op jit(solution)/shard_map/ppermute | solution.py:19
  47.2 7.1 %all-to-all-start.1 = ((bf16[3,128,48,128]{3,1,0,2:T(8,128)(2,1)}), bf16[3,128,48,128]{3,1,0,2:T(8,128)(2,1)}, u32[]{:S(2)}, u32[]{:S(2)}) async-start(bf16[3,128,48,128]{3,1,0,2:T(8,128)(2,1)} %pad_maximum_fusion.3), calls=%async_computation.1 | async-start | bytes 9437184 | tf_op jit(solution)/shard_map/all_to_all | solution.py:43
  54.3 25.9 %collective-permute-done.1 = bf16[2,128,48,128]{3,1,0,2:T(8,128)(2,1)} collective-permute-done((bf16[2,128,48,128]{3,1,0,2:T(8,128)(2,1)S(1)}, bf16[2,128,48,128]{3,1,0,2:T(8,128)(2,1)}, u32[]{:S(2)}, u32[]{:S(2)}) %collective-permute-start.1) | collective-permute-done | bytes 3145760 | tf_op jit(solution)/shard_map/ppermute | solution.py:19
  82.2 36.9 %collective-permute-done.2 = bf16[2,128,48,128]{3,1,0,2:T(8,128)(2,1)S(1)} collective-permute-done((bf16[2,128,48,128]{3,1,0,2:T(8,128)(2,1)}, bf16[2,128,48,128]{3,1,0,2:T(8,128)(2,1)S(1)}, u32[]{:S(2)}, u32[]{:S(2)}) %collective-permute-start.2) | collective-permute-done | bytes 3145760 | tf_op jit(solution)/shard_map/ppermute | solution.py:19
  119.0 6.3 %pad_maximum_fusion = bf16[3,2,128,48,128]{4,2,1,0,3:T(8,128)(2,1)} fusion(bf16[1,2,128,48,128]{4,2,1,0,3:T(8,128)(2,1)S(1)} %bitcast.98, bf16[1,2,128,48,128]{4,2,1,0,3:T(8,128)(2,1)} %bitcast.5, bf16[1,2,128,48,128]{4,2,1,0,3:T(8,128)(2,1)S(1)} %bitcast.99), kind=kLoop, calls=%fused_computation.37 | loop fusion | flops 9437184 | bytes 18874368 | tf_op jit(solution)/shard_map/stack | solution.py:46
  125.4 3.4 all-to-all-done.1
  128.8 5.0 all-to-all-start
  136.1 3.3 copy.65
  141.3 133.8 %all-to-all-done = bf16[3,2,128,48,128]{4,2,1,0,3:T(8,128)(2,1)} async-done(((bf16[3,2,128,48,128]{4,2,1,0,3:T(8,128)(2,1)}), bf16[3,2,128,48,128]{4,2,1,0,3:T(8,128)(2,1)}, u32[]{:S(2)}, u32[]{:S(2)}) %all-to-all-start) | async-done | bytes 9437216 | tf_op jit(solution)/shard_map/all_to_all | solution.py:47
  275.2 11.6 %copy.60 = bf16[3,2,16,128,3,128]{5,3,2,4,1,0:T(8,128)(2,1)} copy(bf16[3,2,16,128,3,128]{5,3,1,0,4,2:T(8,128)(2,1)} %bitcast.9) | data formatting | bytes 18874368 | tf_op jit(solution)/shard_map/all_to_all | solution.py:47
  286.8 6.6 %slice_bitcast_fusion = (bf16[3,3,2048,128]{3,2,0,1:T(8,128)(2,1)S(1)}, bf16[3,3,2048,128]{3,2,0,1:T(8,128)(2,1)}) fusion(bf16[2,3,3,2048,128]{4,3,1,0,2:T(8,128)(2,1)} %bitcast.91), kind=kLoop, calls=%fused_computation.40 | loop fusion | bytes 18874368 | tf_op jit(solution)/shard_map/squeeze | solution.py:55
  293.4 4.0 pad_maximum_fusion.1
  300.5 3.1 copy.67
  303.6 247.9 %while.18 = (s32[]{:T(128)}, f32[3,16,128]{2,1,0:T(8,128)S(1)}, f32[3,16,128]{2,1,0:T(8,128)S(1)}, f32[3,16,128,128]{3,2,1,0:T(8,128)}, s32[16]{0:T(128)S(1)}, /...) while((s32[]{:T(128)}, f32[3,16,128]{2,1,0:T(8,128)S(1)}, ...), condition=%wide.region_3.4_spmd.clone, body=%wide.region_0.3_spmd.clone.sunk | while | flops 415286336 | bytes 27167672 | solution.py:100
  304.4 4.7 gather_fusion.1
  309.1 4.1 bitcast_reduce_fusion.2
  314.4 4.7 gather_fusion.2
  319.1 4.7 fusion.47
  324.6 4.7 gather_fusion.1
  329.3 4.1 bitcast_reduce_fusion.2
  334.6 4.7 gather_fusion.2
  339.3 5.2 fusion.47
  345.3 4.7 gather_fusion.1
  350.0 4.1 bitcast_reduce_fusion.2
  355.3 4.7 gather_fusion.2
  360.0 5.2 fusion.47
  366.0 4.7 gather_fusion.1
  370.7 4.1 bitcast_reduce_fusion.2
  376.0 4.7 gather_fusion.2
  380.7 5.2 fusion.47
  386.7 4.7 gather_fusion.1
  391.4 4.1 bitcast_reduce_fusion.2
  396.7 4.7 gather_fusion.2
  401.4 5.2 fusion.47
  407.4 4.7 gather_fusion.1
  412.1 4.1 bitcast_reduce_fusion.2
  417.4 4.7 gather_fusion.2
  422.1 5.2 fusion.47
  428.1 4.7 gather_fusion.1
  432.8 4.1 bitcast_reduce_fusion.2
  438.1 4.7 gather_fusion.2
  442.8 5.2 fusion.47
  448.8 4.7 gather_fusion.1
  453.5 4.1 bitcast_reduce_fusion.2
  458.8 4.7 gather_fusion.2
  463.5 5.2 fusion.47
  469.5 4.7 gather_fusion.1
  474.2 4.1 bitcast_reduce_fusion.2
  479.5 4.7 gather_fusion.2
  484.2 5.2 fusion.47
  490.2 4.7 gather_fusion.1
  494.9 4.1 bitcast_reduce_fusion.2
  500.2 4.7 gather_fusion.2
  504.9 5.2 fusion.47
  510.9 4.7 gather_fusion.1
  515.6 4.1 bitcast_reduce_fusion.2
  520.9 4.7 gather_fusion.2
  525.6 5.2 fusion.47
  531.6 4.7 gather_fusion.1
  536.3 4.1 bitcast_reduce_fusion.2
  541.6 4.7 gather_fusion.2
  546.3 5.2 fusion.47
  555.3 7.5 %fusion.23 = bf16[3,2048,128]{2,0,1:T(4,128)(2,1)S(1)} fusion(bf16[3,16,128,128]{3,0,2,1:T(4,128)(2,1)S(1)} %copy.68, pred[2048]{0:T(1024)(128)(4,1)S(1)} %iota_compare_fusion), kind=kLoop, calls=%fused_computation.44 | loop fusion | flops 786432 | bytes 3147776 | tf_op jit(solution)/shard_map/convert_element_type | solution.py:106
  562.8 31.7 %all_to_all.54 = bf16[1,2048,3,128]{3,2,0,1:T(4,128)(2,1)S(1)} all-to-all(bf16[1,2048,3,128]{3,2,0,1:T(4,128)(2,1)S(1)} %bitcast.95), channel_id=1, replica_groups=mesh['tm'=16,'space'=16] {'space'}, dimensions={1} | all-to-all | bytes 3145728 | tf_op jit(solution)/shard_map/all_to_all | solution.py:108
  (166 shorter events, 48.9 us)
Async XLA Ops:
  0.0 1.9 copy-start.1
  2.4 41.1 %copy-start.2 = (bf16[1,128,48,128]{3,2,1,0:T(8,128)(2,1)S(1)}, bf16[1,128,48,128]{3,2,1,0:T(8,128)(2,1)}, u32[]{:S(2)}) copy-start(bf16[1,128,48,128]{3,2,1,0:T(8,128)(2,1)} %param.10) | copy-start | bytes 4718596
  2.7 41.2 %copy-start.3 = (bf16[1,128,48,128]{3,2,1,0:T(8,128)(2,1)S(1)}, bf16[1,128,48,128]{3,2,1,0:T(8,128)(2,1)}, u32[]{:S(2)}) copy-start(bf16[1,128,48,128]{3,2,1,0:T(8,128)(2,1)} %param.11) | copy-start | bytes 4718596
  2.7 41.6 %copy-start.4 = (bf16[1,128,48,128]{3,2,1,0:T(8,128)(2,1)S(1)}, bf16[1,128,48,128]{3,2,1,0:T(8,128)(2,1)}, u32[]{:S(2)}) copy-start(bf16[1,128,48,128]{3,2,1,0:T(8,128)(2,1)} %param.12) | copy-start | bytes 4718596
  2.7 38.9 %collective-permute-start = (bf16[2,128,48,128]{3,1,0,2:T(8,128)(2,1)S(1)}, bf16[2,128,48,128]{3,1,0,2:T(8,128)(2,1)S(1)}, u32[]{:S(2)}, u32[]{:S(2)}) collective-permute-start(bf16[2,128,48,128]{3,1,0,2:T(8,128)(2,1)S(1)} %pad_maximum_fusion.4), channel_id=1, source_target_pairs={{0,16},{16,32},{32,48},{48,64},{64,80},{80,96},{96,112},{112,128},... | collective-permute-start | bytes 9437192 | tf_op jit(solution)/shard_map/ppermute | solution.py:19
  41.6 38.7 %collective-permute-start.1 = (bf16[2,128,48,128]{3,1,0,2:T(8,128)(2,1)S(1)}, bf16[2,128,48,128]{3,1,0,2:T(8,128)(2,1)}, u32[]{:S(2)}, u32[]{:S(2)}) collective-permute-start(bf16[2,128,48,128]{3,1,0,2:T(8,128)(2,1)S(1)} %collective-permute-done), channel_id=1, source_target_pairs={{0,16},{16,32},{32,48},{48,64},{64,80},{80,96},{96,112},{112,128},... | collective-permute-start | bytes 9437192 | tf_op jit(solution)/shard_map/ppermute | solution.py:19
  47.2 81.5 %all-to-all-start.1 = ((bf16[3,128,48,128]{3,1,0,2:T(8,128)(2,1)}), bf16[3,128,48,128]{3,1,0,2:T(8,128)(2,1)}, u32[]{:S(2)}, u32[]{:S(2)}) async-start(bf16[3,128,48,128]{3,1,0,2:T(8,128)(2,1)} %pad_maximum_fusion.3), calls=%async_computation.1 | async-start | bytes 9437184 | tf_op jit(solution)/shard_map/all_to_all | solution.py:43
  80.2 38.8 %collective-permute-start.2 = (bf16[2,128,48,128]{3,1,0,2:T(8,128)(2,1)}, bf16[2,128,48,128]{3,1,0,2:T(8,128)(2,1)S(1)}, u32[]{:S(2)}, u32[]{:S(2)}) collective-permute-start(bf16[2,128,48,128]{3,1,0,2:T(8,128)(2,1)} %collective-permute-done.1), channel_id=1, source_target_pairs={{0,16},{16,32},{32,48},{48,64},{64,80},{80,96},{96,112},{112,128},... | collective-permute-start | bytes 9437192 | tf_op jit(solution)/shard_map/ppermute | solution.py:19
  125.3 8.5 %copy-start = (s32[16]{0:T(128)S(1)}, s32[16]{0:T(128)}, u32[]{:S(2)}) copy-start(s32[16]{0:T(128)} %param.17) | copy-start | bytes 196
  125.3 9.4 %copy-start.5 = (s32[1,16,12]{1,0,2:T(1,128)S(1)}, s32[1,16,12]{1,0,2:T(1,128)}, u32[]{:S(2)}) copy-start(s32[1,16,12]{1,0,2:T(1,128)} %param.15) | copy-start | bytes 2308
  128.8 146.4 %all-to-all-start = ((bf16[3,2,128,48,128]{4,2,1,0,3:T(8,128)(2,1)}), bf16[3,2,128,48,128]{4,2,1,0,3:T(8,128)(2,1)}, u32[]{:S(2)}, u32[]{:S(2)}) async-start(bf16[3,2,128,48,128]{4,2,1,0,3:T(8,128)(2,1)} %pad_maximum_fusion), calls=%async_computation | async-start | bytes 18874368 | tf_op jit(solution)/shard_map/all_to_all | solution.py:47
  300.5 3.1 copy-start.6
where the time goes:
time: 599 us; the launch traced here: 597 us
  waiting for transfers between devices  237 us (40%)
  local copies, waits for them, and re-layouts  159 us (27%)
  matrix products  111 us (19%)
  other arithmetic  39.7 us (7%)
  blocking collectives  31.7 us (5%)
  starting transfers between devices  18.1 us (3%)
    all_to_all x1, waiting for transfers between devices, on_device(): lax.all_to_all(stacked, 'space', split_axis=3, concat_axis=2, tiled=True)  134 us
    ppermute x3, waiting for transfers between devices, passed_along(): return lax.ppermute(block, axis, route)  99.5 us
    dot_general x12, matrix products, slot_step(): jnp.einsum('haqk,hakd->haqd', weights.astype(jnp.bfloat16), values_here,...  62.2 us
    gather x12, local copies, waits for them, and re-layouts, slot_step(): keys_here = key_blocks[:, chosen]  56.5 us
    gather x12, local copies, waits for them, and re-layouts, slot_step(): values_here = value_blocks[:, chosen]  56.5 us
    dot_general x12, matrix products, slot_step(): jnp.einsum('haqd,hakd->haqk', query_blocks, keys_here, preferred_element_...  49.1 us
    all_to_all x1, blocking collectives, on_device(): lax.all_to_all(attended_local[None], 'space', split_axis=1, concat_axis=2...  31.7 us
    reduce_sum x12, other arithmetic, slot_step(): row_total = row_total * shrink + jnp.sum(weights, axis=-1)  13.6 us
  transfers between devices with their start and end apart: 5, of which 5 were waited for; matrix products, arithmetic and copies ran while one was open for 3% of the time, Pallas kernels for 0%

commit v1 on v0

v1 whole, which is shorter than its diff:
```python
import functools
import math

import jax
import jax.numpy as jnp
from jax import lax
from jax.experimental import pallas as pl
from jax.experimental.pallas import tpu as pltpu
from jax.sharding import PartitionSpec as P

BLOCK=128; WIN=4; LIST=12; NEG=-1e30
SCALE2 = math.log2(math.e)/math.sqrt(128.0)

def attn_kernel(heads, nb, list_ref, count_ref, live_ref, fresh, p1, p2, p3, out_ref, qbuf, win, sem):
    h = pl.program_id(0)
    def copies(hh, slot):
        yield pltpu.make_async_copy(fresh.at[:, hh, 0], qbuf.at[slot], sem.at[slot, 0])
        yield pltpu.make_async_copy(fresh.at[:, hh, pl.ds(1, 2)], win.at[slot, pl.ds(3*nb, nb)], sem.at[slot, 1])
        for o, p in ((2, p1), (1, p2), (0, p3)):
            yield pltpu.make_async_copy(p.at[:, hh], win.at[slot, pl.ds(o*nb, nb)], sem.at[slot, 2+o])
    for hh in range(heads):
        for c in copies(hh, hh): c.start()
    for hh in range(heads):
        for c in copies(hh, hh): c.wait()
    lane = lax.broadcasted_iota(jnp.int32, (1, 2*BLOCK), 1)
    row = lax.broadcasted_iota(jnp.int32, (BLOCK, 1), 0)

    def make(groups):
        def body(a):
            n = count_ref[a]
            kb, lim = [], []
            for i in range(2*groups):
                e = list_ref[a, i]
                kb.append(e)
                l = jnp.clip(live_ref[lax.shift_right_logical(e, 4)] - (e & (nb-1))*BLOCK, 0, BLOCK)
                lim.append(jnp.where(i < n, l, 0))
            masks = [jnp.where(lane < jnp.where(lane < BLOCK, lim[2*g], lim[2*g+1] + BLOCK), 0.0, NEG) for g in range(groups)]
            qlive = row + a*BLOCK < live_ref[WIN-1]
            for hh in range(heads):
                q = qbuf[hh, a]
                ss = []
                for g in range(groups):
                    k = jnp.concatenate([win[hh, kb[2*g], 0], win[hh, kb[2*g+1], 0]], 0)
                    s = lax.dot_general(q, k, (((1,), (1,)), ((), ())), preferred_element_type=jnp.float32)
                    ss.append(s + masks[g])
                m = functools.reduce(jnp.maximum, ss)
                best = jnp.max(m, axis=1, keepdims=True)
                tot = None; acc = None
                for g in range(groups):
                    w = jnp.exp2((ss[g] - best) * SCALE2)
                    v = jnp.concatenate([win[hh, kb[2*g], 1], win[hh, kb[2*g+1], 1]], 0)
                    r = jnp.dot(w.astype(jnp.bfloat16), v, preferred_element_type=jnp.float32)
                    acc = r if acc is None else acc + r
                    tot = w if tot is None else tot + w
                total = jnp.sum(tot, axis=1, keepdims=True)
                res = acc * (1.0/total)
                out_ref[a, hh] = jnp.where(qlive, res, 0.0).astype(jnp.bfloat16)
        return body
    @pl.loop(0, nb)
    def _(a):
        n = count_ref[a]
        lax.switch((n + 1)//2 - 1, [functools.partial(make(g), a) for g in range(1, LIST//2+1)])

def attention(fresh, p1, p2, p3, lists, counts, live):
    nb, heads = fresh.shape[0], fresh.shape[1]
    D = fresh.shape[-1]
    any_ = pl.BlockSpec(memory_space=pl.ANY)
    return pl.pallas_call(
        functools.partial(attn_kernel, heads, nb),
        out_shape=jax.ShapeDtypeStruct((nb, heads, BLOCK, D), jnp.bfloat16),
        grid_spec=pltpu.PrefetchScalarGridSpec(
            num_scalar_prefetch=3, grid=(1,),
            in_specs=[any_]*4,
            out_specs=pl.BlockSpec((nb, heads, BLOCK, D), lambda i, *_: (0,0,0,0)),
            scratch_shapes=[pltpu.VMEM((heads, nb, BLOCK, D), jnp.bfloat16),
                            pltpu.VMEM((heads, WIN*nb, 2, BLOCK, D), jnp.bfloat16),
                            pltpu.SemaphoreType.DMA((heads, 5))]),
        compiler_params=pltpu.CompilerParams(vmem_limit_bytes=40*2**20),
        cost_estimate=pl.CostEstimate(flops=2*2*heads*nb*6*BLOCK*BLOCK*D, bytes_accessed=16*2**20, transcendentals=heads*nb*6*BLOCK*BLOCK),
    )(lists, counts, live, fresh, p1, p2, p3)


def heads_major(x, parts):
    tokens, heads, size = x.shape[1:]
    return jnp.transpose(x[0], (1, 0, 2)).reshape(parts, heads // parts, tokens, size)


def exchange(x):
    return lax.all_to_all(x, "space", split_axis=0, concat_axis=0, tiled=True)


def next_stretch(x):
    n = lax.axis_size("tm")
    return lax.ppermute(x, "tm", [(i, i + 1) for i in range(n - 1)])


def on_device(queries, noisy_keys, noisy_values, cache_keys, cache_values, block_list, block_count, valid_tokens):
    parts = lax.axis_size("space")
    now = lax.axis_index("tm")
    cache = exchange(jnp.stack([heads_major(x, parts) for x in (cache_keys, cache_values)], 2))
    p1 = next_stretch(cache)
    p2 = next_stretch(p1)
    p3 = next_stretch(p2)
    fresh = exchange(jnp.stack([heads_major(x, parts) for x in (queries, noisy_keys, noisy_values)], 2))
    sources = jnp.maximum(now - (WIN - 1) + jnp.arange(WIN), 0)
    live = valid_tokens[sources]
    out = attention(fresh, p1, p2, p3, block_list[0], block_count[0], live)
    out = exchange(out)
    tokens, size = out.shape[2:]
    return jnp.transpose(out.reshape(-1, tokens, size), (1, 0, 2))[None]


def solution(mesh):
    rows = P("tm", "space", None, None)
    return jax.shard_map(
        on_device,
        mesh=mesh,
        in_specs=(rows,) * 5 + (P("tm", None, None), P("tm", None), P()),
        out_specs=rows,
        check_vma=False,
    )
```

time: 599 us -> 226 us (0.38)
  local copies, waits for them, and re-layouts: 159 us -> 8.45 us
  waiting for transfers between devices: 237 us -> 108 us
  matrix products: 111 us -> 0 us
  blocking collectives: 31.7 us -> 72.4 us
  other arithmetic: 39.7 us -> 2.77 us
  Pallas kernels: 0 us -> 22.1 us
  starting transfers between devices: 18.1 us -> 10.4 us
    gather x37 -> x1, local copies, waits for them, and re-layouts: 121 us -> 0.64 us  [on_device(): live = valid_tokens[sources]]
    dot_general x24 -> x0, matrix products: 111 us -> none  [the longest x12 62.2 us: slot_step(): jnp.einsum('haqk,hakd->haqd', weights.astype(jnp.bfloat16), values_here,...]
    all_to_all x2 -> x1, waiting for transfers between devices: 137 us -> 45.3 us  [exchange(): return lax.all_to_all(x, 'space', split_axis=0, concat_axis=0, tiled=True)]
    all_to_all x1 -> x2, blocking collectives: 31.7 us -> 72.4 us  [exchange(): return lax.all_to_all(x, 'space', split_axis=0, concat_axis=0, tiled=True)]
    ppermute x3, waiting for transfers between devices: 99.5 us -> 63 us  [next_stretch(): return lax.ppermute(x, 'tm', [(i, i + 1) for i in range(n - 1)])]
    pallas_call x0 -> x1, Pallas kernels: none -> 22.1 us  [attention(): pl.pallas_call(functools.partial(attn_kernel, heads, nb), out_shape=jax.S...]
    all_to_all x5 -> x0, local copies, waits for them, and re-layouts: 17.4 us -> none  [the longest x1 11.6 us: on_device(): lax.all_to_all(stacked, 'space', split_axis=3, concat_axis=2, tiled=True)]
    reduce_sum x12 -> x0, other arithmetic: 13.6 us -> none  [slot_step(): row_total = row_total * shrink + jnp.sum(weights, axis=-1)]
  transfers between devices with their start and end apart: 5 -> 4, of which waited for: 5 -> 3; matrix products, arithmetic and copies ran while one was open for 3% -> 2% of each run, Pallas kernels for 0% -> 0%
where the time goes in v1:
time: 226 us; the launch traced here: 225 us
  waiting for transfers between devices  108 us (48%)
  blocking collectives  72.4 us (32%)
  Pallas kernels  22.1 us (10%)
  starting transfers between devices  10.4 us (5%)
  local copies, waits for them, and re-layouts  8.45 us (4%)
  other arithmetic  2.77 us (1%)
    all_to_all x2, blocking collectives, exchange(): return lax.all_to_all(x, 'space', split_axis=0, concat_axis=0, tiled=True)  72.4 us
    ppermute x3, waiting for transfers between devices, next_stretch(): return lax.ppermute(x, 'tm', [(i, i + 1) for i in range(n - 1)])  63 us
    all_to_all x1, waiting for transfers between devices, exchange(): return lax.all_to_all(x, 'space', split_axis=0, concat_axis=0, tiled=True)  45.3 us
    pallas_call x1, Pallas kernels, attention(): pl.pallas_call(functools.partial(attn_kernel, heads, nb), out_shape=jax.S...  22.1 us
    ppermute x3, starting transfers between devices, next_stretch(): return lax.ppermute(x, 'tm', [(i, i + 1) for i in range(n - 1)])  5.73 us
    all_to_all x1, starting transfers between devices, exchange(): return lax.all_to_all(x, 'space', split_axis=0, concat_axis=0, tiled=True)  4.69 us
  transfers between devices with their start and end apart: 4, of which 3 were waited for; matrix products, arithmetic and copies ran while one was open for 2% of the time, Pallas kernels for 0%

profile of v1, /device:TPU:192, one launch (start us, length us, event | category | flops | bytes accessed | tf_op | source)
XLA Modules:
  0.0 224.6 jit_solution(14514225693546689969)
XLA Ops:
  0.0 0.0 copy-start
  0.0 0.0 copy-start.2
  0.0 1.9 copy.20
  1.9 0.0 copy-done.2
  1.9 0.4 copy.21
  2.4 0.3 pad_maximum_fusion.1
  2.7 0.0 copy-start.3
  2.7 46.6 %all_to_all.15 = bf16[16,3,2,128,128]{4,3,2,1,0:T(8,128)(2,1)S(1)} all-to-all(bf16[16,3,2,128,128]{4,3,2,1,0:T(8,128)(2,1)S(1)} %pad_maximum_fusion.1), channel_id=1, replica_groups=mesh['tm'=16,'space'=16] {'space'}, dimensions={0} | all-to-all | bytes 6291456 | tf_op jit(solution)/shard_map/all_to_all | solution.py:89
  49.3 1.9 collective-permute-start
  51.2 36.7 %collective-permute-done.p1 = bf16[16,3,2,128,128]{4,3,2,1,0:T(8,128)(2,1)S(1)} collective-permute-done((bf16[16,3,2,128,128]{4,3,2,1,0:T(8,128)(2,1)S(1)}, bf16[16,3,2,128,128]{4,3,2,1,0:T(8,128)(2,1)S(1)}, u32[]{:S(2)}, u32[]{:S(2)}) %collective-permute-start) | collective-permute-done | bytes 3145760 | tf_op jit(solution)/shard_map/ppermute | solution.py:94
  87.9 1.9 collective-permute-start.1
  89.8 0.0 copy-done.3
  89.8 0.0 copy-start.4
  89.8 0.4 copy.17
  90.2 1.0 copy-done.4
  91.2 0.0 copy-start.5
  91.2 0.4 copy.18
  91.6 1.0 copy-done.5
  92.6 0.4 copy.19
  93.0 2.5 %pad_maximum_fusion = bf16[16,3,3,128,128]{4,3,2,1,0:T(8,128)(2,1)} fusion(bf16[16,3,1,128,128]{4,3,2,1,0:T(8,128)(2,1)S(1)} %bitcast.34, bf16[16,3,1,128,128]{4,3,2,1,0:T(8,128)(2,1)S(1)} %bitcast.33, bf16[16,3,1,128,128]{4,3,2,1,0:T(8,128)(2,1)S(1)} %bitcast.32), kind=kLoop, calls=%fused_computation.1 | loop fusion | flops 4718592 | bytes 9437184 | tf_op jit(solution)/shard_map/stack | solution.py:104
  95.5 0.0 copy-start.6
  95.5 0.0 copy-start.1
  95.5 4.7 %all-to-all-start = ((bf16[16,3,3,128,128]{4,3,2,1,0:T(8,128)(2,1)}), bf16[16,3,3,128,128]{4,3,2,1,0:T(8,128)(2,1)}, u32[]{:S(2)}, u32[]{:S(2)}) async-start(bf16[16,3,3,128,128]{4,3,2,1,0:T(8,128)(2,1)} %pad_maximum_fusion), calls=%async_computation | async-start | bytes 9437184 | tf_op jit(solution)/shard_map/all_to_all | solution.py:89
  100.2 26.4 %collective-permute-done.1.p2 = bf16[16,3,2,128,128]{4,3,2,1,0:T(8,128)(2,1)} collective-permute-done((bf16[16,3,2,128,128]{4,3,2,1,0:T(8,128)(2,1)S(1)}, bf16[16,3,2,128,128]{4,3,2,1,0:T(8,128)(2,1)}, u32[]{:S(2)}, u32[]{:S(2)}) %collective-permute-start.1) | collective-permute-done | bytes 3145760 | tf_op jit(solution)/shard_map/ppermute | solution.py:94
  126.5 1.9 collective-permute-start.2
  128.5 0.0 copy-done.6
  128.5 0.1 copy.16
  128.6 0.0 copy-done
  128.6 0.6 gather_fusion
  129.2 45.3 %all-to-all-done.fresh = bf16[16,3,3,128,128]{4,3,2,1,0:T(8,128)(2,1)} async-done(((bf16[16,3,3,128,128]{4,3,2,1,0:T(8,128)(2,1)}), bf16[16,3,3,128,128]{4,3,2,1,0:T(8,128)(2,1)}, u32[]{:S(2)}, u32[]{:S(2)}) %all-to-all-start) | async-done | bytes 4718624 | tf_op jit(solution)/shard_map/all_to_all | solution.py:89
  174.5 0.0 collective-permute-done.2.p3
  174.5 0.0 copy-done.1
  174.5 22.1 %shard_map.82 = bf16[16,3,128,128]{3,2,1,0:T(8,128)(2,1)S(1)} custom-call(s32[16,12]{1,0:T(8,128)S(1)} %bitcast.30, s32[16]{0:T(128)S(1)} %bitcast.31, s32[4]{0:T(128)S(1)} %gather_fusion, bf16[16,3,3,128,128]{4,3,2,1,0:T(8,128)(2,1)} %all-to-all-done.fresh, bf16[16,3,2,128,128]{4,3,2,1,0:T(8,128)(2,1)S(1)} %collective-permute-done.p1, ...), custom_call_target="tpu_custom_call" | custom-call | flops 2415919104 | bytes 16777216 | tf_op jit(solution)/shard_map/pallas_call | solution.py:68
  196.6 25.8 %all_to_all.16 = bf16[16,3,128,128]{3,2,1,0:T(8,128)(2,1)S(1)} all-to-all(bf16[16,3,128,128]{3,2,1,0:T(8,128)(2,1)S(1)} %shard_map.82), channel_id=1, replica_groups=mesh['tm'=16,'space'=16] {'space'}, dimensions={0} | all-to-all | bytes 3145728 | tf_op jit(solution)/shard_map/all_to_all | solution.py:89
  222.4 2.2 copy.24
  (2 shorter events, 0.0 us)
Async XLA Ops:
  0.0 128.6 %copy-start = (s32[16]{0:T(128)S(1)}, s32[16]{0:T(128)}, u32[]{:S(2)}) copy-start(s32[16]{0:T(128)} %param.15) | copy-start | bytes 196
  0.0 1.9 copy-start.2
  2.7 87.1 %copy-start.3 = (bf16[1,128,48,128]{3,2,1,0:T(8,128)(2,1)S(1)}, bf16[1,128,48,128]{3,2,1,0:T(8,128)(2,1)}, u32[]{:S(2)}) copy-start(bf16[1,128,48,128]{3,2,1,0:T(8,128)(2,1)} %param.8) | copy-start | bytes 4718596
  49.3 38.6 %collective-permute-start = (bf16[16,3,2,128,128]{4,3,2,1,0:T(8,128)(2,1)S(1)}, bf16[16,3,2,128,128]{4,3,2,1,0:T(8,128)(2,1)S(1)}, u32[]{:S(2)}, u32[]{:S(2)}) collective-permute-start(bf16[16,3,2,128,128]{4,3,2,1,0:T(8,128)(2,1)S(1)} %all_to_all.15), channel_id=1, source_target_pairs={{0,16},{16,32},{32,48},{48,64},{64,80},{80,96},{96,112},{112,128},... | collective-permute-start | bytes 9437192 | tf_op jit(solution)/shard_map/ppermute | solution.py:94
  87.9 38.7 %collective-permute-start.1 = (bf16[16,3,2,128,128]{4,3,2,1,0:T(8,128)(2,1)S(1)}, bf16[16,3,2,128,128]{4,3,2,1,0:T(8,128)(2,1)}, u32[]{:S(2)}, u32[]{:S(2)}) collective-permute-start(bf16[16,3,2,128,128]{4,3,2,1,0:T(8,128)(2,1)S(1)} %collective-permute-done.p1), channel_id=1, source_target_pairs={{0,16},{16,32},{32,48},{48,64},{64,80},{80,96},{96,112},{112,128},... | collective-permute-start | bytes 9437192 | tf_op jit(solution)/shard_map/ppermute | solution.py:94
  89.8 1.4 copy-start.4
  91.2 1.4 copy-start.5
  95.5 33.0 %copy-start.6 = (s32[1,16,12]{1,0,2:T(1,128)S(1)}, s32[1,16,12]{1,0,2:T(1,128)}, u32[]{:S(2)}) copy-start(s32[1,16,12]{1,0,2:T(1,128)} %param.13) | copy-start | bytes 2308
  95.5 79.0 %copy-start.1 = (s32[1,16]{1,0:T(1,128)S(1)}, s32[1,16]{1,0:T(1,128)}, u32[]{:S(2)}) copy-start(s32[1,16]{1,0:T(1,128)} %param.14) | copy-start | bytes 196
  95.5 79.0 %all-to-all-start = ((bf16[16,3,3,128,128]{4,3,2,1,0:T(8,128)(2,1)}), bf16[16,3,3,128,128]{4,3,2,1,0:T(8,128)(2,1)}, u32[]{:S(2)}, u32[]{:S(2)}) async-start(bf16[16,3,3,128,128]{4,3,2,1,0:T(8,128)(2,1)} %pad_maximum_fusion), calls=%async_computation | async-start | bytes 9437184 | tf_op jit(solution)/shard_map/all_to_all | solution.py:89
  126.5 47.9 %collective-permute-start.2 = (bf16[16,3,2,128,128]{4,3,2,1,0:T(8,128)(2,1)}, bf16[16,3,2,128,128]{4,3,2,1,0:T(8,128)(2,1)}, u32[]{:S(2)}, u32[]{:S(2)}) collective-permute-start(bf16[16,3,2,128,128]{4,3,2,1,0:T(8,128)(2,1)} %collective-permute-done.1.p2), channel_id=1, source_target_pairs={{0,16},{16,32},{32,48},{48,64},{64,80},{80,96},{96,112},{112,128},... | collective-permute-start | bytes 9437192 | tf_op jit(solution)/shard_map/ppermute | solution.py:94

commit v2 on v1

v2 whole, which is shorter than its diff:
```python
import functools
import math

import jax
import jax.numpy as jnp
from jax import lax
from jax.experimental import pallas as pl
from jax.experimental.pallas import tpu as pltpu
from jax.sharding import PartitionSpec as P

BLOCK = 128
WIN = 4
LIST = 12
NEG = -1e30
SCALE2 = math.log2(math.e) / math.sqrt(128.0)
VMEM_LIMIT = 40 * 2**20


def listed(list_ref, count_ref, pick_ref, size_ref, nb, wanted):
    @pl.loop(0, nb)
    def _(a):
        for i in range(LIST + 1):
            pick_ref[a, i] = (WIN - 1) * nb
        size_ref[a] = 0

        @pl.loop(0, count_ref[a])
        def _(i):
            e = list_ref[a, i]
            k = size_ref[a]
            pick_ref[a, k] = e
            size_ref[a] = k + wanted(e).astype(jnp.int32)


def limits(tab, live_ref, nb):
    token = lax.broadcasted_iota(jnp.int32, (BLOCK, BLOCK), 0)
    tab[0] = jnp.zeros((BLOCK, BLOCK), jnp.float32)
    tab[1] = jnp.full((BLOCK, BLOCK), NEG, jnp.float32)
    for o in range(WIN):
        tab[2 + o] = jnp.where(token < live_ref[o] - (nb - 1) * BLOCK, 0.0, NEG)


def scan(a, groups, pick_ref, size_ref, tab, nb, base, q, keys, values):
    n = size_ref[a]
    kb, kind = [], []
    for i in range(2 * groups):
        e = jnp.where(i < n, pick_ref[a, i], base)
        last = lax.rem(e, nb) == nb - 1
        kb.append(e - base)
        kind.append(jnp.where(i < n, jnp.where(last, 2 + lax.div(e, nb), 0), 1))
    for h in range(len(q)):
        query = q[h]()
        k = jnp.concatenate([keys(h, kb[i]) for i in range(2 * groups)], 0)
        raw = jnp.dot(k, query, preferred_element_type=jnp.float32)
        scores = [raw[i * BLOCK : (i + 1) * BLOCK] + tab[kind[i]] for i in range(2 * groups)]
        best = jnp.max(functools.reduce(jnp.maximum, scores), axis=0, keepdims=True)
        w = [jnp.exp2((s - best) * SCALE2) for s in scores]
        total = functools.reduce(jnp.add, w)
        v = jnp.concatenate([values(h, kb[i]) for i in range(2 * groups)], 1)
        acc = jnp.dot(v, jnp.concatenate([x.astype(jnp.bfloat16) for x in w], 0), preferred_element_type=jnp.float32)
        yield h, best, jnp.sum(total, axis=0, keepdims=True), acc


def near_kernel(where, nb, narr, list_ref, count_ref, live_ref, *refs):
    arrs = refs[:narr]
    acc_ref, stat_ref, qbuf, win, tab, pick, size, sem = refs[narr:]
    heads = len(where)

    def copies(i):
        (fa, fh), pasts = where[i]
        yield pltpu.make_async_copy(arrs[fa].at[:, fh, 0], qbuf.at[i], sem.at[i, 0])
        yield pltpu.make_async_copy(arrs[fa].at[:, fh, pl.ds(1, 2)], win.at[i, pl.ds((WIN - 2) * nb, nb)], sem.at[i, 1])
        for o, (pa, ph) in enumerate(pasts):
            yield pltpu.make_async_copy(arrs[pa].at[:, ph], win.at[i, pl.ds(o * nb, nb)], sem.at[i, 2 + o])

    for i in range(heads):
        for c in copies(i):
            c.start()
    limits(tab, live_ref, nb)
    listed(list_ref, count_ref, pick, size, nb, lambda e: e >= nb)
    for i in range(heads):
        for c in copies(i):
            c.wait()

    def seen(groups, a):
        q = [functools.partial(lambda i: qbuf[i, a], i) for i in range(heads)]
        for h, best, total, acc in scan(
            a, groups, pick, size, tab, nb, nb, q, lambda h, k: win[h, k, 0], lambda h, k: win[h, k, 1]
        ):
            acc_ref[a, h] = acc
            stat_ref[a, h, 0:1] = best
            stat_ref[a, h, 1:2] = total

    @pl.loop(0, nb)
    def _(a):
        lax.switch((size[a] + 1) // 2 - 1, [functools.partial(seen, g, a) for g in range(1, LIST // 2 + 1)])


def far_kernel(where, nb, narr, list_ref, count_ref, live_ref, *refs):
    arrs = refs[:narr]
    acc_ref, stat_ref, out_ref, qbuf, win, acc_buf, stat_buf, tab, pick, size, sem = refs[narr:]
    heads = len(where)

    def copies(i):
        (fa, fh), (pa, ph), sh = where[i]
        yield pltpu.make_async_copy(arrs[fa].at[:, fh, 0], qbuf.at[i], sem.at[i, 0])
        yield pltpu.make_async_copy(arrs[pa].at[:, ph], win.at[i], sem.at[i, 1])
        yield pltpu.make_async_copy(acc_ref.at[:, sh], acc_buf.at[i], sem.at[i, 2])
        yield pltpu.make_async_copy(stat_ref.at[:, sh], stat_buf.at[i], sem.at[i, 3])

    for i in range(heads):
        for c in copies(i):
            c.start()
    limits(tab, live_ref, nb)
    listed(list_ref, count_ref, pick, size, nb, lambda e: e < nb)
    for i in range(heads):
        for c in copies(i):
            c.wait()
    lane = lax.broadcasted_iota(jnp.int32, (1, BLOCK), 1)

    def finish(a, h, acc, total):
        scale = jnp.where(lane < live_ref[WIN - 1] - a * BLOCK, 1.0 / total, 0.0)
        out_ref[a, h] = (acc * scale).astype(jnp.bfloat16)

    def alone(a):
        for h in range(heads):
            finish(a, h, acc_buf[h, a], stat_buf[h, a, 1:2])

    def seen(groups, a):
        q = [functools.partial(lambda i: qbuf[i, a], i) for i in range(heads)]
        for h, best, total, acc in scan(
            a, groups, pick, size, tab, nb, 0, q, lambda h, k: win[h, k, 0], lambda h, k: win[h, k, 1]
        ):
            best0 = stat_buf[h, a, 0:1]
            top = jnp.maximum(best0, best)
            s0 = jnp.exp2((best0 - top) * SCALE2)
            s1 = jnp.exp2((best - top) * SCALE2)
            finish(a, h, acc_buf[h, a] * s0 + acc * s1, stat_buf[h, a, 1:2] * s0 + total * s1)

    @pl.loop(0, nb)
    def _(a):
        n = (size[a] + 1) // 2
        lax.switch(n, [functools.partial(alone, a)] + [functools.partial(seen, g, a) for g in range(1, LIST // 2 + 1)])


def spec(kernel, arrays, scalars, out_shape, scratch):
    nb, _, _, block, size = arrays[0].shape
    whole = [pl.BlockSpec(s.shape, lambda i, *_: (0,) * 4) for s in out_shape]
    heads = out_shape[0].shape[1]
    pairs = heads * nb * LIST // 2
    return pl.pallas_call(
        kernel,
        out_shape=out_shape,
        grid_spec=pltpu.PrefetchScalarGridSpec(
            num_scalar_prefetch=3,
            grid=(1,),
            in_specs=[pl.BlockSpec(memory_space=pl.ANY)] * len(arrays),
            out_specs=whole,
            scratch_shapes=scratch + [pltpu.VMEM((WIN + 2, block, size), jnp.float32), pltpu.SMEM((nb, LIST + 1), jnp.int32), pltpu.SMEM((nb,), jnp.int32), pltpu.SemaphoreType.DMA((heads, 5))],
        ),
        compiler_params=pltpu.CompilerParams(vmem_limit_bytes=VMEM_LIMIT),
        cost_estimate=pl.CostEstimate(
            flops=4 * pairs * block * block * size, bytes_accessed=heads * 5 * 2**20, transcendentals=pairs * block * block
        ),
    )(*scalars, *arrays)


def attend_near(where, arrays, scalars):
    nb, _, _, block, size = arrays[0].shape
    heads = len(where)
    out = [jax.ShapeDtypeStruct((nb, heads, rows, size), jnp.float32) for rows in (block, 8)]
    scratch = [
        pltpu.VMEM((heads, nb, block, size), jnp.bfloat16),
        pltpu.VMEM((heads, (WIN - 1) * nb, 2, block, size), jnp.bfloat16),
    ]
    return spec(functools.partial(near_kernel, where, nb, len(arrays)), arrays, scalars, out, scratch)


def attend_far(where, arrays, state, scalars):
    nb, _, _, block, size = arrays[0].shape
    heads = len(where)
    out = [jax.ShapeDtypeStruct((nb, heads, block, size), jnp.bfloat16)]
    scratch = [
        pltpu.VMEM((heads, nb, block, size), jnp.bfloat16),
        pltpu.VMEM((heads, nb, 2, block, size), jnp.bfloat16),
        pltpu.VMEM((heads, nb, block, size), jnp.float32),
        pltpu.VMEM((heads, nb, 8, size), jnp.float32),
    ]
    return spec(functools.partial(far_kernel, where, nb, len(arrays)), arrays + state, scalars, out, scratch)[0]


def exchange(x):
    return lax.all_to_all(x, "space", split_axis=0, concat_axis=0, tiled=True)


def next_stretch(x):
    n = lax.axis_size("tm")
    return lax.ppermute(x, "tm", [(i, i + 1) for i in range(n - 1)])


GROUPS = ((0,), (1, 2))
FINISH = ((0, 1, 2),)


def on_device(queries, noisy_keys, noisy_values, cache_keys, cache_values, block_list, block_count, valid_tokens):
    parts = lax.axis_size("space")
    now = lax.axis_index("tm")

    def heads_major(x, flip):
        _, heads, _ = x.shape[1:]
        x = jnp.transpose(x[0], (1, 2, 0) if flip else (1, 0, 2))
        return x.reshape(parts, heads // parts, *x.shape[1:])

    own = [heads_major(cache_keys, False), heads_major(cache_values, True)]
    new = [heads_major(queries, True), heads_major(noisy_keys, False), heads_major(noisy_values, True)]
    caches = []
    waiting = [jnp.stack([x[:, g[0] : g[-1] + 1] for x in own], 2) for g in GROUPS] + [jnp.stack(new, 2)]
    for g in range(len(GROUPS)):
        caches.append(exchange(waiting[g]))
        caches[g], *waiting[g + 1 :] = lax.optimization_barrier((caches[g], *waiting[g + 1 :]))
    fresh = exchange(waiting[-1])
    chains = []
    for g, group in enumerate(GROUPS):
        for k in range(len(group)):
            chains.append(caches[g] if len(group) == 1 else caches[g][:, k : k + 1])
    past = []
    for own_cache in chains:
        one = next_stretch(own_cache)
        two = next_stretch(one)
        past.append((next_stretch(two), two, one))
    sources = jnp.maximum(now - (WIN - 1) + jnp.arange(WIN), 0)
    scalars = (block_list[0], block_count[0], valid_tokens[sources])
    count = len(past)
    where = [((0, h), ((1 + 2 * h, 0), (2 + 2 * h, 0))) for h in range(count)]
    arrays = (fresh,) + tuple(x for p in past for x in p[1:])
    state = attend_near(where, arrays, scalars)
    outs = []
    for rest in FINISH:
        where = [((0, h), (1 + i, 0), h) for i, h in enumerate(rest)]
        outs.append(attend_far(where, (fresh,) + tuple(past[h][0] for h in rest), tuple(state), scalars))
    outs = [exchange(o) for o in outs]
    out = outs[0] if len(outs) == 1 else jnp.concatenate(outs, 1)
    size, tokens = out.shape[2:]
    return jnp.transpose(out.reshape(-1, size, tokens), (2, 0, 1))[None]


def solution(mesh):
    rows = P("tm", "space", None, None)
    return jax.shard_map(
        on_device,
        mesh=mesh,
        in_specs=(rows,) * 5 + (P("tm", None, None), P("tm", None), P()),
        out_specs=rows,
        check_vma=False,
    )
```

time: 226 us -> 216 us (0.956)
  the two profiles are of different devices: /device:TPU:192 before, /device:TPU:96 now
where the time goes in v2:
time: 216 us; the launch traced here: 215 us
  waiting for transfers between devices  70.5 us (33%)
  blocking collectives  62.2 us (29%)
  starting transfers between devices  36.8 us (17%)
  Pallas kernels  24.3 us (11%)
  local copies, waits for them, and re-layouts  17.3 us (8%)
  other arithmetic  4.05 us (2%)
    ppermute x9, waiting for transfers between devices, next_stretch(): return lax.ppermute(x, 'tm', [(i, i + 1) for i in range(n - 1)])  64.8 us
    all_to_all x2, blocking collectives, exchange(): return lax.all_to_all(x, 'space', split_axis=0, concat_axis=0, tiled=True)  62.2 us
    ppermute x9, starting transfers between devices, next_stretch(): return lax.ppermute(x, 'tm', [(i, i + 1) for i in range(n - 1)])  25 us
    pallas_call x2, Pallas kernels, spec(): pl.pallas_call(kernel, out_shape=out_shape, grid_spec=pltpu.PrefetchScala...  24.3 us
    all_to_all x2, starting transfers between devices, exchange(): return lax.all_to_all(x, 'space', split_axis=0, concat_axis=0, tiled=True)  11.8 us
    transpose x4, local copies, waits for them, and re-layouts, heads_major(): x = jnp.transpose(x[0], (1, 2, 0) if flip else (1, 0, 2))  8.49 us
    all_to_all x2, waiting for transfers between devices, exchange(): return lax.all_to_all(x, 'space', split_axis=0, concat_axis=0, tiled=True)  5.75 us
  transfers between devices with their start and end apart: 11, of which 9 were waited for; matrix products, arithmetic and copies ran while one was open for 6% of the time, Pallas kernels for 7%

profile of v2, /device:TPU:96, one launch (start us, length us, event | category | flops | bytes accessed | tf_op | source)
XLA Modules:
  0.0 215.5 jit_solution(15857702284368400635)
XLA Ops:
  0.0 0.0 copy-start
  0.0 1.8 copy.31
  1.8 0.0 copy-start.3
  1.8 2.7 %copy.33 = bf16[48,128,128]{2,1,0:T(8,128)(2,1)S(1)} copy(bf16[48,128,128]{1,0,2:T(8,128)(2,1)} %bitcast.51) | data formatting | bytes 3145728 | tf_op jit(solution)/shard_map/transpose | solution.py:210
  4.5 0.0 copy-start.4
  4.6 0.0 copy-done.3
  4.6 0.1 slice_bitcast_fusion.2
  4.7 0.1 pad_maximum_fusion.2
  4.8 0.9 copy-done.4
  5.7 1.0 copy.34
  6.7 0.0 copy-start.5
  6.7 7.2 %all-to-all-start = ((bf16[16,1,2,128,128]{4,3,2,1,0:T(8,128)(2,1)}), bf16[16,1,2,128,128]{4,3,2,1,0:T(8,128)(2,1)}, u32[]{:S(2)}, u32[]{:S(2)}) async-start(bf16[16,1,2,128,128]{4,3,2,1,0:T(8,128)(2,1)} %copy.34), calls=%async_computation | async-start | bytes 2097152 | tf_op jit(solution)/shard_map/all_to_all | solution.py:192
  14.0 0.0 copy-done.5
  14.0 1.1 copy.35
  15.1 1.8 copy.36
  16.9 2.8 %copy.37 = bf16[48,128,128]{2,1,0:T(8,128)(2,1)} copy(bf16[48,128,128]{1,0,2:T(8,128)(2,1)} %bitcast.54) | data formatting | bytes 3145728 | tf_op jit(solution)/shard_map/transpose | solution.py:210
  19.8 1.7 slice_bitcast_fusion
  21.5 0.0 copy-start.2
  21.5 1.5 pad_maximum_fusion.1
  23.0 0.5 copy-done.2
  23.5 2.4 %pad_maximum_fusion = bf16[16,3,3,128,128]{4,3,2,1,0:T(8,128)(2,1)} fusion(bf16[16,3,1,128,128]{4,3,2,1,0:T(8,128)(2,1)S(1)} %bitcast.45, bf16[16,3,1,128,128]{4,3,2,1,0:T(8,128)(2,1)S(1)} %bitcast.44, bf16[16,3,1,128,128]{4,3,2,1,0:T(8,128)(2,1)S(1)} %bitcast.43), kind=kLoop, calls=%fused_computation.1 | loop fusion | flops 4718592 | bytes 9437184 | tf_op jit(solution)/shard_map/stack | solution.py:216
  25.9 5.8 %all-to-all-done = bf16[16,1,2,128,128]{4,3,2,1,0:T(8,128)(2,1)} async-done(((bf16[16,1,2,128,128]{4,3,2,1,0:T(8,128)(2,1)}), bf16[16,1,2,128,128]{4,3,2,1,0:T(8,128)(2,1)}, u32[]{:S(2)}, u32[]{:S(2)}) %all-to-all-start) | async-done | bytes 1048608 | tf_op jit(solution)/shard_map/all_to_all | solution.py:192
  31.7 31.3 %all_to_all.20 = bf16[16,2,2,128,128]{4,3,2,1,0:T(8,128)(2,1)S(1)} all-to-all(bf16[16,2,2,128,128]{4,3,2,1,0:T(8,128)(2,1)} %pad_maximum_fusion.1), channel_id=1, replica_groups=mesh['tm'=16,'space'=16] {'space'}, dimensions={0} | all-to-all | bytes 4194304 | tf_op jit(solution)/shard_map/all_to_all | solution.py:192
  63.0 4.6 %all-to-all-start.2 = ((bf16[16,3,3,128,128]{4,3,2,1,0:T(8,128)(2,1)}), bf16[16,3,3,128,128]{4,3,2,1,0:T(8,128)(2,1)}, u32[]{:S(2)}, u32[]{:S(2)}) async-start(bf16[16,3,3,128,128]{4,3,2,1,0:T(8,128)(2,1)} %pad_maximum_fusion), calls=%async_computation.2 | async-start | bytes 9437184 | tf_op jit(solution)/shard_map/all_to_all | solution.py:192
  67.6 0.0 copy-start.6
  67.6 0.0 copy-start.1
  67.6 2.1 collective-permute-start
  69.7 0.2 fusion
  69.9 5.1 %collective-permute-start.3 = (bf16[16,1,2,128,128]{4,3,2,1,0:T(8,128)(2,1)S(1)}, bf16[16,1,2,128,128]{4,3,2,1,0:T(8,128)(2,1)S(1)}, u32[]{:S(2)}, u32[]{:S(2)}) collective-permute-start(bf16[16,1,2,128,128]{4,3,2,1,0:T(8,128)(2,1)S(1)} %get-tuple-element.20), channel_id=1, source_target_pairs={{0,16},{16,32},{32,48},{48,64},{64,80},{80,96},{96,112},{112,128},... | collective-permute-start | bytes 3145736 | tf_op jit(solution)/shard_map/ppermute | solution.py:197
  75.1 1.9 collective-permute-start.6
  77.0 7.1 %collective-permute-done.refs_2_ = bf16[16,1,2,128,128]{4,3,2,1,0:T(8,128)(2,1)S(1)} collective-permute-done((bf16[16,1,2,128,128]{4,3,2,1,0:T(8,128)(2,1)}, bf16[16,1,2,128,128]{4,3,2,1,0:T(8,128)(2,1)S(1)}, u32[]{:S(2)}, u32[]{:S(2)}) %collective-permute-start) | collective-permute-done | bytes 1048608 | tf_op jit(solution)/shard_map/ppermute | solution.py:197
  84.1 2.8 %collective-permute-start.1 = (bf16[16,1,2,128,128]{4,3,2,1,0:T(8,128)(2,1)S(1)}, bf16[16,1,2,128,128]{4,3,2,1,0:T(8,128)(2,1)}, u32[]{:S(2)}, u32[]{:S(2)}) collective-permute-start(bf16[16,1,2,128,128]{4,3,2,1,0:T(8,128)(2,1)S(1)} %collective-permute-done.refs_2_), channel_id=1, source_target_pairs={{0,16},{16,32},{32,48},{48,64},{64,80},{80,96},{96,112},{112,128},... | collective-permute-start | bytes 3145736 | tf_op jit(solution)/shard_map/ppermute | solution.py:197
  86.8 8.5 %collective-permute-done.3.refs_4_ = bf16[16,1,2,128,128]{4,3,2,1,0:T(8,128)(2,1)S(1)} collective-permute-done((bf16[16,1,2,128,128]{4,3,2,1,0:T(8,128)(2,1)S(1)}, bf16[16,1,2,128,128]{4,3,2,1,0:T(8,128)(2,1)S(1)}, u32[]{:S(2)}, u32[]{:S(2)}) %collective-permute-start.3) | collective-permute-done | bytes 1048608 | tf_op jit(solution)/shard_map/ppermute | solution.py:197
  95.3 2.7 %collective-permute-start.4 = (bf16[16,1,2,128,128]{4,3,2,1,0:T(8,128)(2,1)S(1)}, bf16[16,1,2,128,128]{4,3,2,1,0:T(8,128)(2,1)}, u32[]{:S(2)}, u32[]{:S(2)}) collective-permute-start(bf16[16,1,2,128,128]{4,3,2,1,0:T(8,128)(2,1)S(1)} %collective-permute-done.3.refs_4_), channel_id=1, source_target_pairs={{0,16},{16,32},{32,48},{48,64},{64,80},{80,96},{96,112},{112,128},... | collective-permute-start | bytes 3145736 | tf_op jit(solution)/shard_map/ppermute | solution.py:197
  98.0 8.6 %collective-permute-done.6.refs_6_ = bf16[16,1,2,128,128]{4,3,2,1,0:T(8,128)(2,1)S(1)} collective-permute-done((bf16[16,1,2,128,128]{4,3,2,1,0:T(8,128)(2,1)S(1)}, bf16[16,1,2,128,128]{4,3,2,1,0:T(8,128)(2,1)S(1)}, u32[]{:S(2)}, u32[]{:S(2)}) %collective-permute-start.6) | collective-permute-done | bytes 1048608 | tf_op jit(solution)/shard_map/ppermute | solution.py:197
  106.5 2.7 %collective-permute-start.7 = (bf16[16,1,2,128,128]{4,3,2,1,0:T(8,128)(2,1)S(1)}, bf16[16,1,2,128,128]{4,3,2,1,0:T(8,128)(2,1)}, u32[]{:S(2)}, u32[]{:S(2)}) collective-permute-start(bf16[16,1,2,128,128]{4,3,2,1,0:T(8,128)(2,1)S(1)} %collective-permute-done.6.refs_6_), channel_id=1, source_target_pairs={{0,16},{16,32},{32,48},{48,64},{64,80},{80,96},{96,112},{112,128},... | collective-permute-start | bytes 3145736 | tf_op jit(solution)/shard_map/ppermute | solution.py:197
  109.2 8.7 %collective-permute-done.1.refs_1_ = bf16[16,1,2,128,128]{4,3,2,1,0:T(8,128)(2,1)} collective-permute-done((bf16[16,1,2,128,128]{4,3,2,1,0:T(8,128)(2,1)S(1)}, bf16[16,1,2,128,128]{4,3,2,1,0:T(8,128)(2,1)}, u32[]{:S(2)}, u32[]{:S(2)}) %collective-permute-start.1) | collective-permute-done | bytes 1048608 | tf_op jit(solution)/shard_map/ppermute | solution.py:197
  117.9 2.6 %collective-permute-start.2 = (bf16[16,1,2,128,128]{4,3,2,1,0:T(8,128)(2,1)}, bf16[16,1,2,128,128]{4,3,2,1,0:T(8,128)(2,1)}, u32[]{:S(2)}, u32[]{:S(2)}) collective-permute-start(bf16[16,1,2,128,128]{4,3,2,1,0:T(8,128)(2,1)} %collective-permute-done.1.refs_1_), channel_id=1, source_target_pairs={{0,16},{16,32},{32,48},{48,64},{64,80},{80,96},{96,112},{112,128},... | collective-permute-start | bytes 3145736 | tf_op jit(solution)/shard_map/ppermute | solution.py:197
  120.4 8.7 %collective-permute-done.4.refs_3_ = bf16[16,1,2,128,128]{4,3,2,1,0:T(8,128)(2,1)} collective-permute-done((bf16[16,1,2,128,128]{4,3,2,1,0:T(8,128)(2,1)S(1)}, bf16[16,1,2,128,128]{4,3,2,1,0:T(8,128)(2,1)}, u32[]{:S(2)}, u32[]{:S(2)}) %collective-permute-start.4) | collective-permute-done | bytes 1048608 | tf_op jit(solution)/shard_map/ppermute | solution.py:197
  129.1 2.6 %collective-permute-start.5 = (bf16[16,1,2,128,128]{4,3,2,1,0:T(8,128)(2,1)}, bf16[16,1,2,128,128]{4,3,2,1,0:T(8,128)(2,1)}, u32[]{:S(2)}, u32[]{:S(2)}) collective-permute-start(bf16[16,1,2,128,128]{4,3,2,1,0:T(8,128)(2,1)} %collective-permute-done.4.refs_3_), channel_id=1, source_target_pairs={{0,16},{16,32},{32,48},{48,64},{64,80},{80,96},{96,112},{112,128},... | collective-permute-start | bytes 3145736 | tf_op jit(solution)/shard_map/ppermute | solution.py:197
  131.7 8.7 %collective-permute-done.7.refs_5_ = bf16[16,1,2,128,128]{4,3,2,1,0:T(8,128)(2,1)} collective-permute-done((bf16[16,1,2,128,128]{4,3,2,1,0:T(8,128)(2,1)S(1)}, bf16[16,1,2,128,128]{4,3,2,1,0:T(8,128)(2,1)}, u32[]{:S(2)}, u32[]{:S(2)}) %collective-permute-start.7) | collective-permute-done | bytes 1048608 | tf_op jit(solution)/shard_map/ppermute | solution.py:197
  140.4 2.7 %collective-permute-start.8 = (bf16[16,1,2,128,128]{4,3,2,1,0:T(8,128)(2,1)}, bf16[16,1,2,128,128]{4,3,2,1,0:T(8,128)(2,1)}, u32[]{:S(2)}, u32[]{:S(2)}) collective-permute-start(bf16[16,1,2,128,128]{4,3,2,1,0:T(8,128)(2,1)} %collective-permute-done.7.refs_5_), channel_id=1, source_target_pairs={{0,16},{16,32},{32,48},{48,64},{64,80},{80,96},{96,112},{112,128},... | collective-permute-start | bytes 3145736 | tf_op jit(solution)/shard_map/ppermute | solution.py:197
  143.1 0.0 copy-done.6
  143.1 0.1 copy.30
  143.2 0.0 copy-done
  143.2 0.6 gather_fusion
  143.9 0.0 all-to-all-done.2.refs_0_
  143.9 0.0 copy-done.1
  143.9 15.5 %shard_map.82 = (f32[16,3,128,128]{3,2,1,0:T(8,128)S(1)}, f32[16,3,8,128]{3,2,1,0:T(8,128)S(1)}) custom-call(s32[16,12]{1,0:T(8,128)S(1)} %bitcast.39, s32[16]{0:T(128)S(1)} %bitcast.41, s32[4]{0:T(128)S(1)} %gather_fusion, bf16[16,3,3,128,128]{4,3,2,1,0:T(8,128)(2,1)} %all-to-all-done.2.refs_0_, ...), custom_call_target="tpu_custom_call" | custom-call | flops 2415919104 | bytes 15728640 | tf_op jit(solution)/shard_map/pallas_call | solution.py:150
  159.4 0.0 collective-permute-done.2.refs_1_
  159.4 3.4 %collective-permute-done.5.refs_2_ = bf16[16,1,2,128,128]{4,3,2,1,0:T(8,128)(2,1)} collective-permute-done((bf16[16,1,2,128,128]{4,3,2,1,0:T(8,128)(2,1)}, bf16[16,1,2,128,128]{4,3,2,1,0:T(8,128)(2,1)}, u32[]{:S(2)}, u32[]{:S(2)}) %collective-permute-start.5) | collective-permute-done | bytes 1048608 | tf_op jit(solution)/shard_map/ppermute | solution.py:197
  162.8 11.2 %collective-permute-done.8.refs_3_ = bf16[16,1,2,128,128]{4,3,2,1,0:T(8,128)(2,1)} collective-permute-done((bf16[16,1,2,128,128]{4,3,2,1,0:T(8,128)(2,1)}, bf16[16,1,2,128,128]{4,3,2,1,0:T(8,128)(2,1)}, u32[]{:S(2)}, u32[]{:S(2)}) %collective-permute-start.8) | collective-permute-done | bytes 1048608 | tf_op jit(solution)/shard_map/ppermute | solution.py:197
  174.1 8.8 %shard_map.83 = bf16[16,3,128,128]{3,2,1,0:T(8,128)(2,1)S(1)} custom-call(s32[16,12]{1,0:T(8,128)S(1)} %bitcast.40, s32[16]{0:T(128)S(1)} %bitcast.42, s32[4]{0:T(128)S(1)} %gather_fusion, bf16[16,3,3,128,128]{4,3,2,1,0:T(8,128)(2,1)} %all-to-all-done.2.refs_0_, bf16[16,1,2,128,128]{4,3,2,1,0:T(8,128)(2,1)} %collective-permute-done.2.refs_1_, ...), custom_call_target="tpu_custom_call" | custom-call | flops 2415919104 | bytes 15728640 | tf_op jit(solution)/shard_map/pallas_call | solution.py:150
  182.8 30.9 %all_to_all.21 = bf16[16,3,128,128]{3,2,1,0:T(8,128)(2,1)S(1)} all-to-all(bf16[16,3,128,128]{3,2,1,0:T(8,128)(2,1)S(1)} %shard_map.83), channel_id=1, replica_groups=mesh['tm'=16,'space'=16] {'space'}, dimensions={0} | all-to-all | bytes 3145728 | tf_op jit(solution)/shard_map/all_to_all | solution.py:192
  213.8 1.7 copy.38
  (2 shorter events, 0.0 us)
Async XLA Ops:
  0.0 143.2 %copy-start = (s32[16]{0:T(128)S(1)}, s32[16]{0:T(128)}, u32[]{:S(2)}) copy-start(s32[16]{0:T(128)} %param.15) | copy-start | bytes 196
  1.8 2.7 %copy-start.3 = (bf16[1,128,48,128]{3,1,2,0:T(8,128)(2,1)}, bf16[1,128,48,128]{3,1,2,0:T(8,128)(2,1)S(1)}, u32[]{:S(2)}) copy-start(bf16[1,128,48,128]{3,1,2,0:T(8,128)(2,1)S(1)} %copy.31) | copy-start | bytes 4718596
  4.5 1.2 copy-start.4
  6.7 7.2 %copy-start.5 = (bf16[1,128,48,128]{3,2,1,0:T(8,128)(2,1)S(1)}, bf16[1,128,48,128]{3,2,1,0:T(8,128)(2,1)}, u32[]{:S(2)}) copy-start(bf16[1,128,48,128]{3,2,1,0:T(8,128)(2,1)} %param.8) | copy-start | bytes 4718596
  6.7 25.0 %all-to-all-start = ((bf16[16,1,2,128,128]{4,3,2,1,0:T(8,128)(2,1)}), bf16[16,1,2,128,128]{4,3,2,1,0:T(8,128)(2,1)}, u32[]{:S(2)}, u32[]{:S(2)}) async-start(bf16[16,1,2,128,128]{4,3,2,1,0:T(8,128)(2,1)} %copy.34), calls=%async_computation | async-start | bytes 2097152 | tf_op jit(solution)/shard_map/all_to_all | solution.py:192
  21.5 2.1 copy-start.2
  63.0 80.8 %all-to-all-start.2 = ((bf16[16,3,3,128,128]{4,3,2,1,0:T(8,128)(2,1)}), bf16[16,3,3,128,128]{4,3,2,1,0:T(8,128)(2,1)}, u32[]{:S(2)}, u32[]{:S(2)}) async-start(bf16[16,3,3,128,128]{4,3,2,1,0:T(8,128)(2,1)} %pad_maximum_fusion), calls=%async_computation.2 | async-start | bytes 9437184 | tf_op jit(solution)/shard_map/all_to_all | solution.py:192
  67.6 75.5 %copy-start.6 = (s32[1,16,12]{1,0,2:T(1,128)S(1)}, s32[1,16,12]{1,0,2:T(1,128)}, u32[]{:S(2)}) copy-start(s32[1,16,12]{1,0,2:T(1,128)} %param.13) | copy-start | bytes 2308
  67.6 76.3 %copy-start.1 = (s32[1,16]{1,0:T(1,128)S(1)}, s32[1,16]{1,0:T(1,128)}, u32[]{:S(2)}) copy-start(s32[1,16]{1,0:T(1,128)} %param.14) | copy-start | bytes 196
  67.6 16.5 %collective-permute-start = (bf16[16,1,2,128,128]{4,3,2,1,0:T(8,128)(2,1)}, bf16[16,1,2,128,128]{4,3,2,1,0:T(8,128)(2,1)S(1)}, u32[]{:S(2)}, u32[]{:S(2)}) collective-permute-start(bf16[16,1,2,128,128]{4,3,2,1,0:T(8,128)(2,1)} %all-to-all-done), channel_id=1, source_target_pairs={{0,16},{16,32},{32,48},{48,64},{64,80},{80,96},{96,112},{112,128},... | collective-permute-start | bytes 3145736 | tf_op jit(solution)/shard_map/ppermute | solution.py:197
  69.9 25.4 %collective-permute-start.3 = (bf16[16,1,2,128,128]{4,3,2,1,0:T(8,128)(2,1)S(1)}, bf16[16,1,2,128,128]{4,3,2,1,0:T(8,128)(2,1)S(1)}, u32[]{:S(2)}, u32[]{:S(2)}) collective-permute-start(bf16[16,1,2,128,128]{4,3,2,1,0:T(8,128)(2,1)S(1)} %get-tuple-element.20), channel_id=1, source_target_pairs={{0,16},{16,32},{32,48},{48,64},{64,80},{80,96},{96,112},{112,128},... | collective-permute-start | bytes 3145736 | tf_op jit(solution)/shard_map/ppermute | solution.py:197
  75.1 31.5 %collective-permute-start.6 = (bf16[16,1,2,128,128]{4,3,2,1,0:T(8,128)(2,1)S(1)}, bf16[16,1,2,128,128]{4,3,2,1,0:T(8,128)(2,1)S(1)}, u32[]{:S(2)}, u32[]{:S(2)}) collective-permute-start(bf16[16,1,2,128,128]{4,3,2,1,0:T(8,128)(2,1)S(1)} %get-tuple-element.19), channel_id=1, source_target_pairs={{0,16},{16,32},{32,48},{48,64},{64,80},{80,96},{96,112},{112,128},... | collective-permute-start | bytes 3145736 | tf_op jit(solution)/shard_map/ppermute | solution.py:197
  84.1 33.8 %collective-permute-start.1 = (bf16[16,1,2,128,128]{4,3,2,1,0:T(8,128)(2,1)S(1)}, bf16[16,1,2,128,128]{4,3,2,1,0:T(8,128)(2,1)}, u32[]{:S(2)}, u32[]{:S(2)}) collective-permute-start(bf16[16,1,2,128,128]{4,3,2,1,0:T(8,128)(2,1)S(1)} %collective-permute-done.refs_2_), channel_id=1, source_target_pairs={{0,16},{16,32},{32,48},{48,64},{64,80},{80,96},{96,112},{112,128},... | collective-permute-start | bytes 3145736 | tf_op jit(solution)/shard_map/ppermute | solution.py:197
  95.3 33.8 %collective-permute-start.4 = (bf16[16,1,2,128,128]{4,3,2,1,0:T(8,128)(2,1)S(1)}, bf16[16,1,2,128,128]{4,3,2,1,0:T(8,128)(2,1)}, u32[]{:S(2)}, u32[]{:S(2)}) collective-permute-start(bf16[16,1,2,128,128]{4,3,2,1,0:T(8,128)(2,1)S(1)} %collective-permute-done.3.refs_4_), channel_id=1, source_target_pairs={{0,16},{16,32},{32,48},{48,64},{64,80},{80,96},{96,112},{112,128},... | collective-permute-start | bytes 3145736 | tf_op jit(solution)/shard_map/ppermute | solution.py:197
  106.5 33.8 %collective-permute-start.7 = (bf16[16,1,2,128,128]{4,3,2,1,0:T(8,128)(2,1)S(1)}, bf16[16,1,2,128,128]{4,3,2,1,0:T(8,128)(2,1)}, u32[]{:S(2)}, u32[]{:S(2)}) collective-permute-start(bf16[16,1,2,128,128]{4,3,2,1,0:T(8,128)(2,1)S(1)} %collective-permute-done.6.refs_6_), channel_id=1, source_target_pairs={{0,16},{16,32},{32,48},{48,64},{64,80},{80,96},{96,112},{112,128},... | collective-permute-start | bytes 3145736 | tf_op jit(solution)/shard_map/ppermute | solution.py:197
  117.9 41.5 %collective-permute-start.2 = (bf16[16,1,2,128,128]{4,3,2,1,0:T(8,128)(2,1)}, bf16[16,1,2,128,128]{4,3,2,1,0:T(8,128)(2,1)}, u32[]{:S(2)}, u32[]{:S(2)}) collective-permute-start(bf16[16,1,2,128,128]{4,3,2,1,0:T(8,128)(2,1)} %collective-permute-done.1.refs_1_), channel_id=1, source_target_pairs={{0,16},{16,32},{32,48},{48,64},{64,80},{80,96},{96,112},{112,128},... | collective-permute-start | bytes 3145736 | tf_op jit(solution)/shard_map/ppermute | solution.py:197
  129.1 33.7 %collective-permute-start.5 = (bf16[16,1,2,128,128]{4,3,2,1,0:T(8,128)(2,1)}, bf16[16,1,2,128,128]{4,3,2,1,0:T(8,128)(2,1)}, u32[]{:S(2)}, u32[]{:S(2)}) collective-permute-start(bf16[16,1,2,128,128]{4,3,2,1,0:T(8,128)(2,1)} %collective-permute-done.4.refs_3_), channel_id=1, source_target_pairs={{0,16},{16,32},{32,48},{48,64},{64,80},{80,96},{96,112},{112,128},... | collective-permute-start | bytes 3145736 | tf_op jit(solution)/shard_map/ppermute | solution.py:197
  140.4 33.7 %collective-permute-start.8 = (bf16[16,1,2,128,128]{4,3,2,1,0:T(8,128)(2,1)}, bf16[16,1,2,128,128]{4,3,2,1,0:T(8,128)(2,1)}, u32[]{:S(2)}, u32[]{:S(2)}) collective-permute-start(bf16[16,1,2,128,128]{4,3,2,1,0:T(8,128)(2,1)} %collective-permute-done.7.refs_5_), channel_id=1, source_target_pairs={{0,16},{16,32},{32,48},{48,64},{64,80},{80,96},{96,112},{112,128},... | collective-permute-start | bytes 3145736 | tf_op jit(solution)/shard_map/ppermute | solution.py:197

commit v3 on v2

--- a/solution.py
+++ b/solution.py
@@ -13,7 +13,7 @@
 LIST = 12
 NEG = -1e30
 SCALE2 = math.log2(math.e) / math.sqrt(128.0)
-VMEM_LIMIT = 40 * 2**20
+VMEM_LIMIT = 26 * 2**20
 
 
 def listed(list_ref, count_ref, pick_ref, size_ref, nb, wanted):
@@ -47,16 +47,27 @@
         last = lax.rem(e, nb) == nb - 1
         kb.append(e - base)
         kind.append(jnp.where(i < n, jnp.where(last, 2 + lax.div(e, nb), 0), 1))
-    for h in range(len(q)):
+    heads = range(len(q))
+    halves = [range(half * groups, (half + 1) * groups) for half in range(2)]
+    scores = []
+    for h in heads:
         query = q[h]()
-        k = jnp.concatenate([keys(h, kb[i]) for i in range(2 * groups)], 0)
-        raw = jnp.dot(k, query, preferred_element_type=jnp.float32)
-        scores = [raw[i * BLOCK : (i + 1) * BLOCK] + tab[kind[i]] for i in range(2 * groups)]
-        best = jnp.max(functools.reduce(jnp.maximum, scores), axis=0, keepdims=True)
-        w = [jnp.exp2((s - best) * SCALE2) for s in scores]
+        raw = [
+            jnp.dot(jnp.concatenate([keys(h, kb[i]) for i in part], 0), query, preferred_element_type=jnp.float32)
+            for part in halves
+        ]
+        scores.append([raw[i // groups][(i % groups) * BLOCK : (i % groups + 1) * BLOCK] + tab[kind[i]] for i in range(2 * groups)])
+    bests = [jnp.max(functools.reduce(jnp.maximum, scores[h]), axis=0, keepdims=True) for h in heads]
+    for h in heads:
+        best = bests[h]
+        w = [jnp.exp2((s - best) * SCALE2) for s in scores[h]]
         total = functools.reduce(jnp.add, w)
-        v = jnp.concatenate([values(h, kb[i]) for i in range(2 * groups)], 1)
-        acc = jnp.dot(v, jnp.concatenate([x.astype(jnp.bfloat16) for x in w], 0), preferred_element_type=jnp.float32)
+        acc = None
+        for part in halves:
+            v = jnp.concatenate([values(h, kb[i]) for i in part], 1)
+            p = jnp.concatenate([w[i].astype(jnp.bfloat16) for i in part], 0)
+            r = jnp.dot(v, p, preferred_element_type=jnp.float32)
+            acc = r if acc is None else acc + r
         yield h, best, jnp.sum(total, axis=0, keepdims=True), acc
 
 
@@ -83,9 +94,10 @@
 
     def seen(groups, a):
         q = [functools.partial(lambda i: qbuf[i, a], i) for i in range(heads)]
-        for h, best, total, acc in scan(
+        found = list(scan(
             a, groups, pick, size, tab, nb, nb, q, lambda h, k: win[h, k, 0], lambda h, k: win[h, k, 1]
-        ):
+        ))
+        for h, best, total, acc in found:
             acc_ref[a, h] = acc
             stat_ref[a, h, 0:1] = best
             stat_ref[a, h, 1:2] = total
@@ -127,9 +139,10 @@
 
     def seen(groups, a):
         q = [functools.partial(lambda i: qbuf[i, a], i) for i in range(heads)]
-        for h, best, total, acc in scan(
+        found = list(scan(
             a, groups, pick, size, tab, nb, 0, q, lambda h, k: win[h, k, 0], lambda h, k: win[h, k, 1]
-        ):
+        ))
+        for h, best, total, acc in found:
             best0 = stat_buf[h, a, 0:1]
             top = jnp.maximum(best0, best)
             s0 = jnp.exp2((best0 - top) * SCALE2)
@@ -197,6 +210,10 @@
     return lax.ppermute(x, "tm", [(i, i + 1) for i in range(n - 1)])
 
 
+def moved(x, route):
+    return lax.ppermute(x, "tm", route)
+
+
 GROUPS = ((0,), (1, 2))
 FINISH = ((0, 1, 2),)
 
@@ -207,13 +224,14 @@
 
     def heads_major(x, flip):
         _, heads, _ = x.shape[1:]
-        x = jnp.transpose(x[0], (1, 2, 0) if flip else (1, 0, 2))
-        return x.reshape(parts, heads // parts, *x.shape[1:])
+        slots = [x[0][:, k : k + parts] for k in range(0, heads, parts)]
+        return [jnp.transpose(s, (1, 2, 0) if flip else (1, 0, 2)) for s in slots]
 
     own = [heads_major(cache_keys, False), heads_major(cache_values, True)]
     new = [heads_major(queries, True), heads_major(noisy_keys, False), heads_major(noisy_values, True)]
     caches = []
-    waiting = [jnp.stack([x[:, g[0] : g[-1] + 1] for x in own], 2) for g in GROUPS] + [jnp.stack(new, 2)]
+    waiting = [jnp.stack([jnp.stack([x[k] for x in own], 1) for k in g], 1) for g in GROUPS]
+    waiting.append(jnp.stack([jnp.stack([x[k] for x in new], 1) for k in range(len(new[0]))], 1))
     for g in range(len(GROUPS)):
         caches.append(exchange(waiting[g]))
         caches[g], *waiting[g + 1 :] = lax.optimization_barrier((caches[g], *waiting[g + 1 :]))
@@ -223,7 +241,17 @@
         for k in range(len(group)):
             chains.append(caches[g] if len(group) == 1 else caches[g][:, k : k + 1])
     past = []
-    for own_cache in chains:
+    pairs = lax.axis_size("tm")
+    for h, own_cache in enumerate(chains):
+        if h == 0:
+            one = next_stretch(own_cache)
+            cross = moved(own_cache, [(i, i + 3) for i in range(0, pairs - 3, 2)])
+            ahead = moved(one, [(i, i + 2) for i in range(0, pairs - 2, 2)])
+            even = lax.rem(now, 2) == 0
+            swap = [(i, i + 1) for i in range(0, pairs, 2)] + [(i + 1, i) for i in range(0, pairs, 2)]
+            two = moved(jnp.where(even, one, cross), swap)
+            past.append((jnp.where(even, ahead, cross), two, one))
+            continue
         one = next_stretch(own_cache)
         two = next_stretch(one)
         past.append((next_stretch(two), two, one))
@@ -239,8 +267,8 @@
         outs.append(attend_far(where, (fresh,) + tuple(past[h][0] for h in rest), tuple(state), scalars))
     outs = [exchange(o) for o in outs]
     out = outs[0] if len(outs) == 1 else jnp.concatenate(outs, 1)
-    size, tokens = out.shape[2:]
-    return jnp.transpose(out.reshape(-1, size, tokens), (2, 0, 1))[None]
+    out = jnp.transpose(out, (3, 1, 0, 2))
+    return out.reshape(1, out.shape[0], -1, out.shape[3])
 
 
 def solution(mesh):

time: 216 us -> 216 us (level)
  the two profiles are of different devices: /device:TPU:96 before, /device:TPU:97 now
where the time goes in v3:
time: 216 us
  blocking collectives  60 us (28%)
  waiting for transfers between devices  52.9 us (24%)
  starting transfers between devices  49.1 us (23%)
  Pallas kernels  26.1 us (12%)
  local copies, waits for them, and re-layouts  21.4 us (10%)
  other arithmetic  5.82 us (3%)
    all_to_all x2, blocking collectives, exchange(): return lax.all_to_all(x, 'space', split_axis=0, concat_axis=0, tiled=True)  60 us
    ppermute x7, waiting for transfers between devices, next_stretch(): return lax.ppermute(x, 'tm', [(i, i + 1) for i in range(n - 1)])  50.9 us
    ppermute x7, starting transfers between devices, next_stretch(): return lax.ppermute(x, 'tm', [(i, i + 1) for i in range(n - 1)])  34.6 us
    pallas_call x2, Pallas kernels, spec(): pl.pallas_call(kernel, out_shape=out_shape, grid_spec=pltpu.PrefetchScala...  26.1 us
    unnamed x32, local copies, waits for them, and re-layouts  13.5 us
    all_to_all x2, starting transfers between devices, exchange(): return lax.all_to_all(x, 'space', split_axis=0, concat_axis=0, tiled=True)  11.5 us
  transfers between devices with their start and end apart: 12, of which 6 were waited for; matrix products, arithmetic and copies ran while one was open for 6% of the time, Pallas kernels for 8%

profile of v3, /device:TPU:97, one launch (start us, length us, event | category | flops | bytes accessed | tf_op | source)
XLA Modules:
  0.0 215.6 jit_solution(942712708271587439)
XLA Ops:
  0.0 1.8 copy.63
  1.8 0.9 slice_bitcast_fusion.12
  2.8 2.1 copy.42
  4.9 1.1 slice_bitcast_fusion.11
  6.0 0.1 maximum_bitcast_fusion.3
  6.1 1.0 copy.43
  7.2 6.8 %all-to-all-start = ((bf16[16,1,2,128,128]{4,3,2,1,0:T(8,128)(2,1)}), bf16[16,1,2,128,128]{4,3,2,1,0:T(8,128)(2,1)}, u32[]{:S(2)}, u32[]{:S(2)}) async-start(bf16[16,1,2,128,128]{4,3,2,1,0:T(8,128)(2,1)} %copy.43), calls=%async_computation | async-start | bytes 2097152 | tf_op jit(solution)/shard_map/all_to_all | solution.py:205
  14.0 2.1 copy.46
  16.1 0.0 copy-start.10
  16.1 0.9 slice_bitcast_fusion.8
  17.1 0.6 copy-done.10
  17.7 0.4 copy.62
  18.1 1.2 slice_bitcast_fusion.7
  19.3 2.1 copy.48
  21.5 0.1 slice_bitcast_fusion.6
  21.6 0.9 copy-done.6
  22.5 0.2 copy-done.7
  22.6 0.2 maximum_bitcast_fusion.2
  22.8 0.9 copy-done.5
  23.7 0.1 maximum_bitcast_fusion.5
  23.8 0.1 copy-done.8
  23.9 0.2 copy-done.9
  24.0 0.1 pad_maximum_fusion.1
  24.2 0.9 copy-done.3
  25.1 0.2 copy-done.4
  25.2 0.3 maximum_bitcast_fusion
  25.6 2.5 %pad_maximum_fusion = bf16[16,3,3,128,128]{4,3,2,1,0:T(8,128)(2,1)} fusion(bf16[16,1,3,128,128]{4,3,2,1,0:T(8,128)(2,1)S(1)} %maximum_bitcast_fusion.2, bf16[16,1,3,128,128]{4,3,0,2,1:T(8,128)(2,1)S(1)} %get-tuple-element.38, bf16[16,1,3,128,128]{4,3,0,2,1:T(8,128)(2,1)S(1)} %get-tuple-element.39), kind=kLoop, calls=%fused_computation.1 | loop fusion | flops 14155776 | bytes 9437184 | tf_op jit(solution)/shard_map/stack | solution.py:234
  28.1 2.0 all-to-all-done
  30.1 31.6 %all_to_all.20 = bf16[16,2,2,128,128]{4,3,2,1,0:T(8,128)(2,1)} all-to-all(bf16[16,2,2,128,128]{4,3,2,1,0:T(8,128)(2,1)S(1)} %pad_maximum_fusion.1), channel_id=1, replica_groups=mesh['tm'=16,'space'=16] {'space'}, dimensions={0} | all-to-all | bytes 4194304 | tf_op jit(solution)/shard_map/all_to_all | solution.py:205
  61.7 4.7 %all-to-all-start.2 = ((bf16[16,3,3,128,128]{4,3,2,1,0:T(8,128)(2,1)}), bf16[16,3,3,128,128]{4,3,2,1,0:T(8,128)(2,1)}, u32[]{:S(2)}, u32[]{:S(2)}) async-start(bf16[16,3,3,128,128]{4,3,2,1,0:T(8,128)(2,1)} %pad_maximum_fusion), calls=%async_computation.2 | async-start | bytes 9437184 | tf_op jit(solution)/shard_map/all_to_all | solution.py:205
  66.4 7.0 %collective-permute-start = (bf16[16,1,2,128,128]{4,3,2,1,0:T(8,128)(2,1)}, bf16[16,1,2,128,128]{4,3,2,1,0:T(8,128)(2,1)S(1)}, u32[]{:S(2)}, u32[]{:S(2)}) collective-permute-start(bf16[16,1,2,128,128]{4,3,2,1,0:T(8,128)(2,1)} %all-to-all-done), channel_id=1, source_target_pairs={{0,16},{16,32},{32,48},{48,64},{64,80},{80,96},{96,112},{112,128},... | collective-permute-start | bytes 3145736 | tf_op jit(solution)/shard_map/ppermute | solution.py:210
  73.4 0.1 fusion
  73.5 1.9 collective-permute-start.6
  75.4 3.0 %collective-permute-start.3 = (bf16[16,1,2,128,128]{4,3,2,1,0:T(8,128)(2,1)S(1)}, bf16[16,1,2,128,128]{4,3,2,1,0:T(8,128)(2,1)}, u32[]{:S(2)}, u32[]{:S(2)}) collective-permute-start(bf16[16,1,2,128,128]{4,3,2,1,0:T(8,128)(2,1)S(1)} %get-tuple-element.20), channel_id=1, source_target_pairs={{0,16},{16,32},{32,48},{48,64},{64,80},{80,96},{96,112},{112,128},... | collective-permute-start | bytes 3145736 | tf_op jit(solution)/shard_map/ppermute | solution.py:210
  78.5 1.3 collective-permute-start.2
  79.8 8.5 %collective-permute-done.refs_2_ = bf16[16,1,2,128,128]{4,3,2,1,0:T(8,128)(2,1)S(1)} collective-permute-done((bf16[16,1,2,128,128]{4,3,2,1,0:T(8,128)(2,1)}, bf16[16,1,2,128,128]{4,3,2,1,0:T(8,128)(2,1)S(1)}, u32[]{:S(2)}, u32[]{:S(2)}) %collective-permute-start) | collective-permute-done | bytes 1048608 | tf_op jit(solution)/shard_map/ppermute | solution.py:210
  88.3 1.6 collective-permute-start.1
  89.9 20.7 %collective-permute-done.6.refs_6_ = bf16[16,1,2,128,128]{4,3,2,1,0:T(8,128)(2,1)S(1)} collective-permute-done((bf16[16,1,2,128,128]{4,3,2,1,0:T(8,128)(2,1)S(1)}, bf16[16,1,2,128,128]{4,3,2,1,0:T(8,128)(2,1)S(1)}, u32[]{:S(2)}, u32[]{:S(2)}) %collective-permute-start.6) | collective-permute-done | bytes 1048608 | tf_op jit(solution)/shard_map/ppermute | solution.py:210
  110.6 5.6 %collective-permute-start.7 = (bf16[16,1,2,128,128]{4,3,2,1,0:T(8,128)(2,1)S(1)}, bf16[16,1,2,128,128]{4,3,2,1,0:T(8,128)(2,1)}, u32[]{:S(2)}, u32[]{:S(2)}) collective-permute-start(bf16[16,1,2,128,128]{4,3,2,1,0:T(8,128)(2,1)S(1)} %collective-permute-done.6.refs_6_), channel_id=1, source_target_pairs={{0,16},{16,32},{32,48},{48,64},{64,80},{80,96},{96,112},{112,128},... | collective-permute-start | bytes 3145736 | tf_op jit(solution)/shard_map/ppermute | solution.py:210
  116.2 14.0 %collective-permute-done.3.refs_4_ = bf16[16,1,2,128,128]{4,3,2,1,0:T(8,128)(2,1)} collective-permute-done((bf16[16,1,2,128,128]{4,3,2,1,0:T(8,128)(2,1)S(1)}, bf16[16,1,2,128,128]{4,3,2,1,0:T(8,128)(2,1)}, u32[]{:S(2)}, u32[]{:S(2)}) %collective-permute-start.3) | collective-permute-done | bytes 1048608 | tf_op jit(solution)/shard_map/ppermute | solution.py:210
  130.2 5.7 %collective-permute-start.4 = (bf16[16,1,2,128,128]{4,3,2,1,0:T(8,128)(2,1)}, bf16[16,1,2,128,128]{4,3,2,1,0:T(8,128)(2,1)}, u32[]{:S(2)}, u32[]{:S(2)}) collective-permute-start(bf16[16,1,2,128,128]{4,3,2,1,0:T(8,128)(2,1)} %collective-permute-done.3.refs_4_), channel_id=1, source_target_pairs={{0,16},{16,32},{32,48},{48,64},{64,80},{80,96},{96,112},{112,128},... | collective-permute-start | bytes 3145736 | tf_op jit(solution)/shard_map/ppermute | solution.py:210
  135.9 0.0 copy-start.12
  135.9 0.0 copy-start.1
  136.0 0.0 collective-permute-done.2
  136.0 0.0 copy-start.11
  136.0 1.0 copy-done.11
  136.9 0.0 collective-permute-done.1
  136.9 2.5 %broadcast_select_fusion = (bf16[16,1,2,128,128]{4,3,2,1,0:T(8,128)(2,1)}, bf16[16,1,2,128,128]{4,3,2,1,0:T(8,128)(2,1)S(1)}) fusion(bf16[16,1,2,128,128]{4,3,2,1,0:T(8,128)(2,1)S(1)} %collective-permute-done.refs_2_, bf16[16,1,2,128,128]{4,3,2,1,0:T(8,128)(2,1)} %copy-done.11, pred[]{:T(512)S(6)} %eq.3, bf16[16,1,2,128,128]{4,3,2,1,0:T(8,128)(2,1)} %collective-permute-done.1), kind=kLoop, calls=%fused_computation.11 | loop fusion | flops 1048576 | bytes 5242881 | tf_op jit(solution)/shard_map/jit(_where)/select_n | solution.py:252
  139.4 0.0 collective-permute-start.9
  139.4 2.0 collective-permute-done.7.refs_5_
  141.5 5.7 %collective-permute-start.8 = (bf16[16,1,2,128,128]{4,3,2,1,0:T(8,128)(2,1)}, bf16[16,1,2,128,128]{4,3,2,1,0:T(8,128)(2,1)}, u32[]{:S(2)}, u32[]{:S(2)}) collective-permute-start(bf16[16,1,2,128,128]{4,3,2,1,0:T(8,128)(2,1)} %collective-permute-done.7.refs_5_), channel_id=1, source_target_pairs={{0,16},{16,32},{32,48},{48,64},{64,80},{80,96},{96,112},{112,128},... | collective-permute-start | bytes 3145736 | tf_op jit(solution)/shard_map/ppermute | solution.py:210
  147.2 5.6 %collective-permute-done.4.refs_3_ = bf16[16,1,2,128,128]{4,3,2,1,0:T(8,128)(2,1)} collective-permute-done((bf16[16,1,2,128,128]{4,3,2,1,0:T(8,128)(2,1)}, bf16[16,1,2,128,128]{4,3,2,1,0:T(8,128)(2,1)}, u32[]{:S(2)}, u32[]{:S(2)}) %collective-permute-start.4) | collective-permute-done | bytes 1048608 | tf_op jit(solution)/shard_map/ppermute | solution.py:210
  152.8 5.8 %collective-permute-start.5 = (bf16[16,1,2,128,128]{4,3,2,1,0:T(8,128)(2,1)}, bf16[16,1,2,128,128]{4,3,2,1,0:T(8,128)(2,1)}, u32[]{:S(2)}, u32[]{:S(2)}) collective-permute-start(bf16[16,1,2,128,128]{4,3,2,1,0:T(8,128)(2,1)} %collective-permute-done.4.refs_3_), channel_id=1, source_target_pairs={{0,16},{16,32},{32,48},{48,64},{64,80},{80,96},{96,112},{112,128},... | collective-permute-start | bytes 3145736 | tf_op jit(solution)/shard_map/ppermute | solution.py:210
  158.6 0.1 copy.40
  158.7 0.0 copy-done
  158.7 0.6 gather_fusion
  159.3 0.0 collective-permute-done.9.refs_1_
  159.3 0.0 all-to-all-done.2.refs_0_
  159.4 17.5 %shard_map.82 = (f32[16,3,128,128]{3,2,1,0:T(8,128)S(1)}, f32[16,3,8,128]{3,2,1,0:T(8,128)S(1)}) custom-call(s32[16,12]{1,0:T(8,128)S(1)} %bitcast.95, s32[16]{0:T(128)S(1)} %bitcast.97, s32[4]{0:T(128)S(1)} %gather_fusion, bf16[16,3,3,128,128]{4,3,2,1,0:T(8,128)(2,1)} %all-to-all-done.2.refs_0_, ...), custom_call_target="tpu_custom_call" | custom-call | flops 2415919104 | bytes 15728640 | tf_op jit(solution)/shard_map/pallas_call | solution.py:163
  176.9 0.0 collective-permute-done.8.refs_3_
  176.9 0.0 collective-permute-done.5.refs_2_
  176.9 8.6 %shard_map.83 = bf16[16,3,128,128]{3,2,1,0:T(8,128)(2,1)S(1)} custom-call(s32[16,12]{1,0:T(8,128)S(1)} %bitcast.96, s32[16]{0:T(128)S(1)} %bitcast.98, s32[4]{0:T(128)S(1)} %gather_fusion, bf16[16,3,3,128,128]{4,3,2,1,0:T(8,128)(2,1)} %all-to-all-done.2.refs_0_, bf16[16,1,2,128,128]{4,3,2,1,0:T(8,128)(2,1)S(1)} %get-tuple-element.37.refs_1_, ...), custom_call_target="tpu_custom_call" | custom-call | flops 2415919104 | bytes 15728640 | tf_op jit(solution)/shard_map/pallas_call | solution.py:163
  185.5 28.4 %all_to_all.21 = bf16[16,3,128,128]{3,2,1,0:T(8,128)(2,1)S(1)} all-to-all(bf16[16,3,128,128]{3,2,1,0:T(8,128)(2,1)S(1)} %shard_map.83), channel_id=1, replica_groups=mesh['tm'=16,'space'=16] {'space'}, dimensions={0} | all-to-all | bytes 3145728 | tf_op jit(solution)/shard_map/all_to_all | solution.py:205
  213.9 1.7 copy.53
  (14 shorter events, 0.0 us)
Async XLA Ops:
  0.0 158.7 %copy-start = (s32[16]{0:T(128)S(1)}, s32[16]{0:T(128)}, u32[]{:S(2)}) copy-start(s32[16]{0:T(128)} %param.15) | copy-start | bytes 196
  7.2 22.9 %all-to-all-start = ((bf16[16,1,2,128,128]{4,3,2,1,0:T(8,128)(2,1)}), bf16[16,1,2,128,128]{4,3,2,1,0:T(8,128)(2,1)}, u32[]{:S(2)}, u32[]{:S(2)}) async-start(bf16[16,1,2,128,128]{4,3,2,1,0:T(8,128)(2,1)} %copy.43), calls=%async_computation | async-start | bytes 2097152 | tf_op jit(solution)/shard_map/all_to_all | solution.py:205
  16.1 1.6 copy-start.10
  21.4 1.0 copy-start.6
  21.4 1.2 copy-start.7
  22.6 1.0 copy-start.5
  22.8 1.1 copy-start.8
  22.8 1.2 copy-start.9
  24.0 1.0 copy-start.3
  24.0 1.2 copy-start.4
  61.7 11.7 %copy-start.2 = (bf16[16,2,2,128,128]{4,3,2,1,0:T(8,128)(2,1)S(1)}, bf16[16,2,2,128,128]{4,3,2,1,0:T(8,128)(2,1)}, u32[]{:S(2)}) copy-start(bf16[16,2,2,128,128]{4,3,2,1,0:T(8,128)(2,1)} %all_to_all.20) | copy-start | bytes 6291460
  61.7 97.7 %all-to-all-start.2 = ((bf16[16,3,3,128,128]{4,3,2,1,0:T(8,128)(2,1)}), bf16[16,3,3,128,128]{4,3,2,1,0:T(8,128)(2,1)}, u32[]{:S(2)}, u32[]{:S(2)}) async-start(bf16[16,3,3,128,128]{4,3,2,1,0:T(8,128)(2,1)} %pad_maximum_fusion), calls=%async_computation.2 | async-start | bytes 9437184 | tf_op jit(solution)/shard_map/all_to_all | solution.py:205
  66.4 21.9 %collective-permute-start = (bf16[16,1,2,128,128]{4,3,2,1,0:T(8,128)(2,1)}, bf16[16,1,2,128,128]{4,3,2,1,0:T(8,128)(2,1)S(1)}, u32[]{:S(2)}, u32[]{:S(2)}) collective-permute-start(bf16[16,1,2,128,128]{4,3,2,1,0:T(8,128)(2,1)} %all-to-all-done), channel_id=1, source_target_pairs={{0,16},{16,32},{32,48},{48,64},{64,80},{80,96},{96,112},{112,128},... | collective-permute-start | bytes 3145736 | tf_op jit(solution)/shard_map/ppermute | solution.py:210
  73.5 37.1 %collective-permute-start.6 = (bf16[16,1,2,128,128]{4,3,2,1,0:T(8,128)(2,1)S(1)}, bf16[16,1,2,128,128]{4,3,2,1,0:T(8,128)(2,1)S(1)}, u32[]{:S(2)}, u32[]{:S(2)}) collective-permute-start(bf16[16,1,2,128,128]{4,3,2,1,0:T(8,128)(2,1)S(1)} %get-tuple-element.19), channel_id=1, source_target_pairs={{0,16},{16,32},{32,48},{48,64},{64,80},{80,96},{96,112},{112,128},... | collective-permute-start | bytes 3145736 | tf_op jit(solution)/shard_map/ppermute | solution.py:210
  75.4 54.8 %collective-permute-start.3 = (bf16[16,1,2,128,128]{4,3,2,1,0:T(8,128)(2,1)S(1)}, bf16[16,1,2,128,128]{4,3,2,1,0:T(8,128)(2,1)}, u32[]{:S(2)}, u32[]{:S(2)}) collective-permute-start(bf16[16,1,2,128,128]{4,3,2,1,0:T(8,128)(2,1)S(1)} %get-tuple-element.20), channel_id=1, source_target_pairs={{0,16},{16,32},{32,48},{48,64},{64,80},{80,96},{96,112},{112,128},... | collective-permute-start | bytes 3145736 | tf_op jit(solution)/shard_map/ppermute | solution.py:210
  78.5 57.5 %collective-permute-start.2 = (bf16[16,1,2,128,128]{4,3,2,1,0:T(8,128)(2,1)}, bf16[16,1,2,128,128]{4,3,2,1,0:T(8,128)(2,1)S(1)}, u32[]{:S(2)}, u32[]{:S(2)}) collective-permute-start(bf16[16,1,2,128,128]{4,3,2,1,0:T(8,128)(2,1)} %all-to-all-done), channel_id=1, source_target_pairs={{0,48},{32,80},{64,112},{96,144},{128,176},{160,208},{192,240},{1,... | collective-permute-start | bytes 3145736 | tf_op jit(solution)/shard_map/ppermute | solution.py:214
  88.3 48.7 %collective-permute-start.1 = (bf16[16,1,2,128,128]{4,3,2,1,0:T(8,128)(2,1)S(1)}, bf16[16,1,2,128,128]{4,3,2,1,0:T(8,128)(2,1)}, u32[]{:S(2)}, u32[]{:S(2)}) collective-permute-start(bf16[16,1,2,128,128]{4,3,2,1,0:T(8,128)(2,1)S(1)} %collective-permute-done.refs_2_), channel_id=1, source_target_pairs={{0,32},{32,64},{64,96},{96,128},{128,160},{160,192},{192,224},{1,3... | collective-permute-start | bytes 3145736 | tf_op jit(solution)/shard_map/ppermute | solution.py:214
  110.6 30.8 %collective-permute-start.7 = (bf16[16,1,2,128,128]{4,3,2,1,0:T(8,128)(2,1)S(1)}, bf16[16,1,2,128,128]{4,3,2,1,0:T(8,128)(2,1)}, u32[]{:S(2)}, u32[]{:S(2)}) collective-permute-start(bf16[16,1,2,128,128]{4,3,2,1,0:T(8,128)(2,1)S(1)} %collective-permute-done.6.refs_6_), channel_id=1, source_target_pairs={{0,16},{16,32},{32,48},{48,64},{64,80},{80,96},{96,112},{112,128},... | collective-permute-start | bytes 3145736 | tf_op jit(solution)/shard_map/ppermute | solution.py:210
  130.2 22.6 %collective-permute-start.4 = (bf16[16,1,2,128,128]{4,3,2,1,0:T(8,128)(2,1)}, bf16[16,1,2,128,128]{4,3,2,1,0:T(8,128)(2,1)}, u32[]{:S(2)}, u32[]{:S(2)}) collective-permute-start(bf16[16,1,2,128,128]{4,3,2,1,0:T(8,128)(2,1)} %collective-permute-done.3.refs_4_), channel_id=1, source_target_pairs={{0,16},{16,32},{32,48},{48,64},{64,80},{80,96},{96,112},{112,128},... | collective-permute-start | bytes 3145736 | tf_op jit(solution)/shard_map/ppermute | solution.py:210
  135.9 22.7 %copy-start.12 = (s32[1,16,12]{1,0,2:T(1,128)S(1)}, s32[1,16,12]{1,0,2:T(1,128)}, u32[]{:S(2)}) copy-start(s32[1,16,12]{1,0,2:T(1,128)} %param.13) | copy-start | bytes 2308
  135.9 23.4 %copy-start.1 = (s32[1,16]{1,0:T(1,128)S(1)}, s32[1,16]{1,0:T(1,128)}, u32[]{:S(2)}) copy-start(s32[1,16]{1,0:T(1,128)} %param.14) | copy-start | bytes 196
  136.0 1.0 copy-start.11
  139.4 19.9 %collective-permute-start.9 = (bf16[16,1,2,128,128]{4,3,2,1,0:T(8,128)(2,1)}, bf16[16,1,2,128,128]{4,3,2,1,0:T(8,128)(2,1)}, u32[]{:S(2)}, u32[]{:S(2)}) collective-permute-start(bf16[16,1,2,128,128]{4,3,2,1,0:T(8,128)(2,1)} %get-tuple-element.36), channel_id=1, source_target_pairs={{0,16},{32,48},{64,80},{96,112},{128,144},{160,176},{192,208},{224... | collective-permute-start | bytes 3145736 | tf_op jit(solution)/shard_map/ppermute | solution.py:214
  141.5 35.4 %collective-permute-start.8 = (bf16[16,1,2,128,128]{4,3,2,1,0:T(8,128)(2,1)}, bf16[16,1,2,128,128]{4,3,2,1,0:T(8,128)(2,1)}, u32[]{:S(2)}, u32[]{:S(2)}) collective-permute-start(bf16[16,1,2,128,128]{4,3,2,1,0:T(8,128)(2,1)} %collective-permute-done.7.refs_5_), channel_id=1, source_target_pairs={{0,16},{16,32},{32,48},{48,64},{64,80},{80,96},{96,112},{112,128},... | collective-permute-start | bytes 3145736 | tf_op jit(solution)/shard_map/ppermute | solution.py:210
  152.8 24.1 %collective-permute-start.5 = (bf16[16,1,2,128,128]{4,3,2,1,0:T(8,128)(2,1)}, bf16[16,1,2,128,128]{4,3,2,1,0:T(8,128)(2,1)}, u32[]{:S(2)}, u32[]{:S(2)}) collective-permute-start(bf16[16,1,2,128,128]{4,3,2,1,0:T(8,128)(2,1)} %collective-permute-done.4.refs_3_), channel_id=1, source_target_pairs={{0,16},{16,32},{32,48},{48,64},{64,80},{80,96},{96,112},{112,128},... | collective-permute-start | bytes 3145736 | tf_op jit(solution)/shard_map/ppermute | solution.py:210

commit v4 on v3

--- a/solution.py
+++ b/solution.py
@@ -222,20 +222,26 @@
     parts = lax.axis_size("space")
     now = lax.axis_index("tm")
 
-    def heads_major(x, flip):
+    def heads_major(x, flip, first=False):
         _, heads, _ = x.shape[1:]
         slots = [x[0][:, k : k + parts] for k in range(0, heads, parts)]
+        if first:
+            slots[0] = lax.dynamic_slice_in_dim(x[0], lax.div(now, lax.axis_size("tm")), parts, 1)
         return [jnp.transpose(s, (1, 2, 0) if flip else (1, 0, 2)) for s in slots]
 
-    own = [heads_major(cache_keys, False), heads_major(cache_values, True)]
+    own = [heads_major(cache_keys, False, True), heads_major(cache_values, True, True)]
+    waiting = [jnp.stack([jnp.stack([x[k] for x in own], 1) for k in g], 1) for g in GROUPS]
+    caches = [exchange(waiting[0])]
+    sources = jnp.maximum(now - (WIN - 1) + jnp.arange(WIN), 0)
+    scalars = (block_list[0], block_count[0], valid_tokens[sources])
+    caches[0], waiting[1], queries, noisy_keys, noisy_values, scalars = lax.optimization_barrier(
+        (caches[0], waiting[1], queries, noisy_keys, noisy_values, scalars)
+    )
+    caches.append(exchange(waiting[1]))
     new = [heads_major(queries, True), heads_major(noisy_keys, False), heads_major(noisy_values, True)]
-    caches = []
-    waiting = [jnp.stack([jnp.stack([x[k] for x in own], 1) for k in g], 1) for g in GROUPS]
-    waiting.append(jnp.stack([jnp.stack([x[k] for x in new], 1) for k in range(len(new[0]))], 1))
-    for g in range(len(GROUPS)):
-        caches.append(exchange(waiting[g]))
-        caches[g], *waiting[g + 1 :] = lax.optimization_barrier((caches[g], *waiting[g + 1 :]))
-    fresh = exchange(waiting[-1])
+    new = jnp.stack([jnp.stack([x[k] for x in new], 1) for k in range(len(new[0]))], 1)
+    caches[1], new = lax.optimization_barrier((caches[1], new))
+    fresh = exchange(new)
     chains = []
     for g, group in enumerate(GROUPS):
         for k in range(len(group)):
@@ -255,8 +261,6 @@
         one = next_stretch(own_cache)
         two = next_stretch(one)
         past.append((next_stretch(two), two, one))
-    sources = jnp.maximum(now - (WIN - 1) + jnp.arange(WIN), 0)
-    scalars = (block_list[0], block_count[0], valid_tokens[sources])
     count = len(past)
     where = [((0, h), ((1 + 2 * h, 0), (2 + 2 * h, 0))) for h in range(count)]
     arrays = (fresh,) + tuple(x for p in past for x in p[1:])

time: 216 us -> 215 us (level)
  blocking collectives: 60 us -> 27.7 us
  waiting for transfers between devices: 52.9 us -> 75.3 us
  starting transfers between devices: 49.1 us -> 55.4 us
    all_to_all x2 -> x1, blocking collectives: 60 us -> 27.7 us  [exchange(): return lax.all_to_all(x, 'space', split_axis=0, concat_axis=0, tiled=True)]
    all_to_all x2 -> x3, waiting for transfers between devices: 1.99 us -> 23.4 us  [exchange(): return lax.all_to_all(x, 'space', split_axis=0, concat_axis=0, tiled=True)]
    optimization_barrier x0 -> x3, local copies, waits for them, and re-layouts: none -> 8.67 us  [on_device(): lax.optimization_barrier((caches[0], waiting[1], queries, noisy_keys, noi...]
    unnamed x32 -> x23, local copies, waits for them, and re-layouts: 13.5 us -> 7.37 us
    all_to_all x2 -> x3, starting transfers between devices: 11.5 us -> 17.6 us  [exchange(): return lax.all_to_all(x, 'space', split_axis=0, concat_axis=0, tiled=True)]
    dynamic_slice x0 -> x3, local copies, waits for them, and re-layouts: none -> 2.48 us  [heads_major(): lax.dynamic_slice_in_dim(x[0], lax.div(now, lax.axis_size('tm')), parts, 1)]
    another operation x3, other arithmetic: 0.34 us -> 2.66 us  [on_device(): jnp.stack([jnp.stack([x[k] for x in own], 1) for k in g], 1)]
  transfers between devices with their start and end apart: 12 -> 13, of which waited for: 6 -> 7; matrix products, arithmetic and copies ran while one was open for 6% -> 9% of each run, Pallas kernels for 8% -> 8%
where the time goes in v4:
time: 215 us; the launch traced here: 214 us
  waiting for transfers between devices  75.3 us (35%)
  starting transfers between devices  55.4 us (26%)
  blocking collectives  27.7 us (13%)
  Pallas kernels  25.4 us (12%)
  local copies, waits for them, and re-layouts  23 us (11%)
  other arithmetic  6.79 us (3%)
    ppermute x7, waiting for transfers between devices, next_stretch(): return lax.ppermute(x, 'tm', [(i, i + 1) for i in range(n - 1)])  51.9 us
    ppermute x7, starting transfers between devices, next_stretch(): return lax.ppermute(x, 'tm', [(i, i + 1) for i in range(n - 1)])  34.8 us
    all_to_all x1, blocking collectives, exchange(): return lax.all_to_all(x, 'space', split_axis=0, concat_axis=0, tiled=True)  27.7 us
    pallas_call x2, Pallas kernels, spec(): pl.pallas_call(kernel, out_shape=out_shape, grid_spec=pltpu.PrefetchScala...  25.4 us
    all_to_all x3, waiting for transfers between devices, exchange(): return lax.all_to_all(x, 'space', split_axis=0, concat_axis=0, tiled=True)  23.4 us
    all_to_all x3, starting transfers between devices, exchange(): return lax.all_to_all(x, 'space', split_axis=0, concat_axis=0, tiled=True)  17.6 us
    optimization_barrier x3, local copies, waits for them, and re-layouts, on_device(): lax.optimization_barrier((caches[0], waiting[1], queries, noisy_keys, noi...  8.67 us
    unnamed x23, local copies, waits for them, and re-layouts  7.37 us
  transfers between devices with their start and end apart: 13, of which 7 were waited for; matrix products, arithmetic and copies ran while one was open for 9% of the time, Pallas kernels for 8%

profile of v4, /device:TPU:97, one launch (start us, length us, event | category | flops | bytes accessed | tf_op | source)
XLA Modules:
  0.0 213.9 jit_solution(3447567129933590951)
XLA Ops:
  0.0 1.9 constant_dynamic-slice_fusion
  1.9 0.5 copy.24
  2.3 0.1 copy.49
  2.5 1.1 maximum_bitcast_fusion.3
  3.6 6.9 %all-to-all-start = ((bf16[16,1,2,128,128]{4,3,2,1,0:T(8,128)(2,1)}), bf16[16,1,2,128,128]{4,3,2,1,0:T(8,128)(2,1)}, u32[]{:S(2)}, u32[]{:S(2)}) async-start(bf16[16,1,2,128,128]{4,3,2,1,0:T(8,128)(2,1)} %maximum_bitcast_fusion.3), calls=%async_computation | async-start | bytes 2097152 | tf_op jit(solution)/shard_map/all_to_all | solution.py:205
  10.5 0.4 copy.48
  10.9 0.0 copy-start.9
  11.0 2.1 copy.26
  13.1 0.0 copy-done.9
  13.1 0.1 copy.29
  13.2 0.6 gather_fusion
  13.8 0.1 slice_bitcast_fusion.12
  13.9 0.1 slice_bitcast_fusion.11
  14.0 0.1 maximum_bitcast_fusion.5
  14.1 1.5 pad_maximum_fusion.1
  15.6 11.0 %all-to-all-done = bf16[16,1,2,128,128]{4,3,2,1,0:T(8,128)(2,1)} async-done(((bf16[16,1,2,128,128]{4,3,2,1,0:T(8,128)(2,1)}), bf16[16,1,2,128,128]{4,3,2,1,0:T(8,128)(2,1)}, u32[]{:S(2)}, u32[]{:S(2)}) %all-to-all-start) | async-done | bytes 1048608 | tf_op jit(solution)/shard_map/all_to_all | solution.py:205
  26.6 4.2 %all-to-all-start.1 = ((bf16[16,2,2,128,128]{4,3,2,1,0:T(8,128)(2,1)}), bf16[16,2,2,128,128]{4,3,2,1,0:T(8,128)(2,1)S(1)}, u32[]{:S(2)}, u32[]{:S(2)}) async-start(bf16[16,2,2,128,128]{4,3,2,1,0:T(8,128)(2,1)} %pad_maximum_fusion.1), calls=%async_computation.1 | async-start | bytes 4194304 | tf_op jit(solution)/shard_map/all_to_all | solution.py:205
  30.8 2.9 %copy.30 = bf16[1,128,48,128]{1,3,2,0:T(8,128)(2,1)} copy(bf16[1,128,48,128]{3,2,1,0:T(8,128)(2,1)} %param.8) | data formatting | bytes 3145728 | tf_op jit(solution)/shard_map/optimization_barrier | solution.py:237
  33.7 3.0 %copy.47 = bf16[1,128,48,128]{3,1,2,0:T(8,128)(2,1)} copy(bf16[1,128,48,128]{3,2,1,0:T(8,128)(2,1)} %param.9) | data formatting | bytes 3145728 | tf_op jit(solution)/shard_map/optimization_barrier | solution.py:237
  36.7 2.8 %copy.32 = bf16[1,128,48,128]{1,3,2,0:T(8,128)(2,1)} copy(bf16[1,128,48,128]{3,2,1,0:T(8,128)(2,1)} %param.10) | data formatting | bytes 3145728 | tf_op jit(solution)/shard_map/optimization_barrier | solution.py:237
  39.5 1.6 slice_bitcast_fusion.8
  41.1 0.3 copy-done.6
  41.4 0.1 slice_bitcast_fusion.7
  41.5 1.3 copy-done.5
  42.8 0.1 slice_bitcast_fusion.6
  42.9 0.2 maximum_bitcast_fusion.2
  43.1 0.2 maximum_bitcast_fusion.1
  43.2 2.4 %pad_maximum_fusion = bf16[16,3,3,128,128]{4,3,2,1,0:T(8,128)(2,1)} fusion(bf16[16,1,3,128,128]{4,3,2,1,0:T(8,128)(2,1)S(1)} %maximum_bitcast_fusion.2, bf16[16,1,128,128]{3,2,0,1:T(8,128)(2,1)S(1)} %get-tuple-element.37, bf16[16,1,128,128]{3,2,0,1:T(8,128)(2,1)S(1)} %get-tuple-element.34, bf16[16,1,128,128]{3,2,0,1:T(8,128)(2,1)S(1)} %get-tuple-element.31, ...), kind=kLoop, calls=%fused_computation.1 | loop fusion | flops 15728640 | bytes 9437184 | tf_op jit(solution)/shard_map/stack | solution.py:242
  45.6 12.4 %all-to-all-done.1 = bf16[16,2,2,128,128]{4,3,2,1,0:T(8,128)(2,1)S(1)} async-done(((bf16[16,2,2,128,128]{4,3,2,1,0:T(8,128)(2,1)}), bf16[16,2,2,128,128]{4,3,2,1,0:T(8,128)(2,1)S(1)}, u32[]{:S(2)}, u32[]{:S(2)}) %all-to-all-start.1) | async-done | bytes 2097184 | tf_op jit(solution)/shard_map/all_to_all | solution.py:205
  58.0 6.4 %all-to-all-start.2 = ((bf16[16,3,3,128,128]{4,3,2,1,0:T(8,128)(2,1)}), bf16[16,3,3,128,128]{4,3,2,1,0:T(8,128)(2,1)}, u32[]{:S(2)}, u32[]{:S(2)}) async-start(bf16[16,3,3,128,128]{4,3,2,1,0:T(8,128)(2,1)} %pad_maximum_fusion), calls=%async_computation.2 | async-start | bytes 9437184 | tf_op jit(solution)/shard_map/all_to_all | solution.py:205
  64.5 7.1 %collective-permute-start = (bf16[16,1,2,128,128]{4,3,2,1,0:T(8,128)(2,1)}, bf16[16,1,2,128,128]{4,3,2,1,0:T(8,128)(2,1)S(1)}, u32[]{:S(2)}, u32[]{:S(2)}) collective-permute-start(bf16[16,1,2,128,128]{4,3,2,1,0:T(8,128)(2,1)} %all-to-all-done), channel_id=1, source_target_pairs={{0,16},{16,32},{32,48},{48,64},{64,80},{80,96},{96,112},{112,128},... | collective-permute-start | bytes 3145736 | tf_op jit(solution)/shard_map/ppermute | solution.py:210
  71.6 0.1 fusion
  71.8 1.9 collective-permute-start.6
  73.7 3.0 %collective-permute-start.3 = (bf16[16,1,2,128,128]{4,3,2,1,0:T(8,128)(2,1)S(1)}, bf16[16,1,2,128,128]{4,3,2,1,0:T(8,128)(2,1)}, u32[]{:S(2)}, u32[]{:S(2)}) collective-permute-start(bf16[16,1,2,128,128]{4,3,2,1,0:T(8,128)(2,1)S(1)} %get-tuple-element.30), channel_id=1, source_target_pairs={{0,16},{16,32},{32,48},{48,64},{64,80},{80,96},{96,112},{112,128},... | collective-permute-start | bytes 3145736 | tf_op jit(solution)/shard_map/ppermute | solution.py:210
  76.7 1.3 collective-permute-start.2
  78.0 8.5 %collective-permute-done.refs_2_ = bf16[16,1,2,128,128]{4,3,2,1,0:T(8,128)(2,1)S(1)} collective-permute-done((bf16[16,1,2,128,128]{4,3,2,1,0:T(8,128)(2,1)}, bf16[16,1,2,128,128]{4,3,2,1,0:T(8,128)(2,1)S(1)}, u32[]{:S(2)}, u32[]{:S(2)}) %collective-permute-start) | collective-permute-done | bytes 1048608 | tf_op jit(solution)/shard_map/ppermute | solution.py:210
  86.5 1.6 collective-permute-start.1
  88.2 20.7 %collective-permute-done.6.refs_6_ = bf16[16,1,2,128,128]{4,3,2,1,0:T(8,128)(2,1)S(1)} collective-permute-done((bf16[16,1,2,128,128]{4,3,2,1,0:T(8,128)(2,1)S(1)}, bf16[16,1,2,128,128]{4,3,2,1,0:T(8,128)(2,1)S(1)}, u32[]{:S(2)}, u32[]{:S(2)}) %collective-permute-start.6) | collective-permute-done | bytes 1048608 | tf_op jit(solution)/shard_map/ppermute | solution.py:210
  108.9 5.6 %collective-permute-start.7 = (bf16[16,1,2,128,128]{4,3,2,1,0:T(8,128)(2,1)S(1)}, bf16[16,1,2,128,128]{4,3,2,1,0:T(8,128)(2,1)}, u32[]{:S(2)}, u32[]{:S(2)}) collective-permute-start(bf16[16,1,2,128,128]{4,3,2,1,0:T(8,128)(2,1)S(1)} %collective-permute-done.6.refs_6_), channel_id=1, source_target_pairs={{0,16},{16,32},{32,48},{48,64},{64,80},{80,96},{96,112},{112,128},... | collective-permute-start | bytes 3145736 | tf_op jit(solution)/shard_map/ppermute | solution.py:210
  114.5 14.0 %collective-permute-done.3.refs_4_ = bf16[16,1,2,128,128]{4,3,2,1,0:T(8,128)(2,1)} collective-permute-done((bf16[16,1,2,128,128]{4,3,2,1,0:T(8,128)(2,1)S(1)}, bf16[16,1,2,128,128]{4,3,2,1,0:T(8,128)(2,1)}, u32[]{:S(2)}, u32[]{:S(2)}) %collective-permute-start.3) | collective-permute-done | bytes 1048608 | tf_op jit(solution)/shard_map/ppermute | solution.py:210
  128.5 5.7 %collective-permute-start.4 = (bf16[16,1,2,128,128]{4,3,2,1,0:T(8,128)(2,1)}, bf16[16,1,2,128,128]{4,3,2,1,0:T(8,128)(2,1)}, u32[]{:S(2)}, u32[]{:S(2)}) collective-permute-start(bf16[16,1,2,128,128]{4,3,2,1,0:T(8,128)(2,1)} %collective-permute-done.3.refs_4_), channel_id=1, source_target_pairs={{0,16},{16,32},{32,48},{48,64},{64,80},{80,96},{96,112},{112,128},... | collective-permute-start | bytes 3145736 | tf_op jit(solution)/shard_map/ppermute | solution.py:210
  134.2 0.0 copy-start.4
  134.2 0.0 collective-permute-done.2
  134.2 0.0 copy-start.8
  134.2 1.0 copy-done.8
  135.2 0.0 collective-permute-done.1
  135.2 1.4 broadcast_select_fusion
  136.6 0.1 collective-permute-start.9
  136.7 3.0 %collective-permute-done.7.refs_5_ = bf16[16,1,2,128,128]{4,3,2,1,0:T(8,128)(2,1)} collective-permute-done((bf16[16,1,2,128,128]{4,3,2,1,0:T(8,128)(2,1)S(1)}, bf16[16,1,2,128,128]{4,3,2,1,0:T(8,128)(2,1)}, u32[]{:S(2)}, u32[]{:S(2)}) %collective-permute-start.7) | collective-permute-done | bytes 1048608 | tf_op jit(solution)/shard_map/ppermute | solution.py:210
  139.7 5.7 %collective-permute-start.8 = (bf16[16,1,2,128,128]{4,3,2,1,0:T(8,128)(2,1)}, bf16[16,1,2,128,128]{4,3,2,1,0:T(8,128)(2,1)}, u32[]{:S(2)}, u32[]{:S(2)}) collective-permute-start(bf16[16,1,2,128,128]{4,3,2,1,0:T(8,128)(2,1)} %collective-permute-done.7.refs_5_), channel_id=1, source_target_pairs={{0,16},{16,32},{32,48},{48,64},{64,80},{80,96},{96,112},{112,128},... | collective-permute-start | bytes 3145736 | tf_op jit(solution)/shard_map/ppermute | solution.py:210
  145.4 5.6 %collective-permute-done.4.refs_3_ = bf16[16,1,2,128,128]{4,3,2,1,0:T(8,128)(2,1)} collective-permute-done((bf16[16,1,2,128,128]{4,3,2,1,0:T(8,128)(2,1)}, bf16[16,1,2,128,128]{4,3,2,1,0:T(8,128)(2,1)}, u32[]{:S(2)}, u32[]{:S(2)}) %collective-permute-start.4) | collective-permute-done | bytes 1048608 | tf_op jit(solution)/shard_map/ppermute | solution.py:210
  151.1 5.8 %collective-permute-start.5 = (bf16[16,1,2,128,128]{4,3,2,1,0:T(8,128)(2,1)}, bf16[16,1,2,128,128]{4,3,2,1,0:T(8,128)(2,1)}, u32[]{:S(2)}, u32[]{:S(2)}) collective-permute-start(bf16[16,1,2,128,128]{4,3,2,1,0:T(8,128)(2,1)} %collective-permute-done.4.refs_3_), channel_id=1, source_target_pairs={{0,16},{16,32},{32,48},{48,64},{64,80},{80,96},{96,112},{112,128},... | collective-permute-start | bytes 3145736 | tf_op jit(solution)/shard_map/ppermute | solution.py:210
  156.8 0.0 collective-permute-done.9.refs_1_
  156.9 0.0 copy-start.2
  156.9 1.0 copy-done.2
  157.8 0.0 all-to-all-done.2.refs_0_
  157.8 1.2 copy-done.3
  159.1 16.9 %shard_map.82 = (f32[16,3,128,128]{3,2,1,0:T(8,128)S(1)}, f32[16,3,8,128]{3,2,1,0:T(8,128)S(1)}) custom-call(s32[16,12]{1,0:T(8,128)S(1)} %bitcast.101, s32[16]{0:T(128)S(1)} %bitcast.103, s32[4]{0:T(128)S(1)} %gather_fusion, bf16[16,3,3,128,128]{4,3,2,1,0:T(8,128)(2,1)} %all-to-all-done.2.refs_0_, bf16[16,1,2,128,128]{4,3,2,1,0:T(8,128)(2,1)S(1)} %copy-done.3, ...), custom_call_target="tpu_custom_call" | custom-call | flops 2415919104 | bytes 15728640 | tf_op jit(solution)/shard_map/pallas_call | solution.py:163
  176.0 0.0 collective-permute-done.8.refs_3_
  176.0 0.0 collective-permute-done.5.refs_2_
  176.0 8.5 %shard_map.83 = bf16[16,3,128,128]{3,2,1,0:T(8,128)(2,1)S(1)} custom-call(s32[16,12]{1,0:T(8,128)S(1)} %bitcast.102, s32[16]{0:T(128)S(1)} %bitcast.104, s32[4]{0:T(128)S(1)} %gather_fusion, bf16[16,3,3,128,128]{4,3,2,1,0:T(8,128)(2,1)} %all-to-all-done.2.refs_0_, bf16[16,1,2,128,128]{4,3,2,1,0:T(8,128)(2,1)S(1)} %get-tuple-element.45.refs_1_, ...), custom_call_target="tpu_custom_call" | custom-call | flops 2415919104 | bytes 15728640 | tf_op jit(solution)/shard_map/pallas_call | solution.py:163
  184.5 27.7 %all_to_all.20 = bf16[16,3,128,128]{3,2,1,0:T(8,128)(2,1)S(1)} all-to-all(bf16[16,3,128,128]{3,2,1,0:T(8,128)(2,1)S(1)} %shard_map.83), channel_id=1, replica_groups=mesh['tm'=16,'space'=16] {'space'}, dimensions={0} | all-to-all | bytes 3145728 | tf_op jit(solution)/shard_map/all_to_all | solution.py:205
  212.2 1.7 copy.37
  213.9 0.0 copy-done.1
  (11 shorter events, 0.0 us)
Async XLA Ops:
  0.0 13.2 %copy-start = (s32[16]{0:T(128)S(1)}, s32[16]{0:T(128)}, u32[]{:S(2)}) copy-start(s32[16]{0:T(128)} %param.15) | copy-start | bytes 196
  3.6 7.0 %copy-start.7 = (bf16[1,128,48,128]{3,2,1,0:T(8,128)(2,1)S(1)}, bf16[1,128,48,128]{3,2,1,0:T(8,128)(2,1)}, u32[]{:S(2)}) copy-start(bf16[1,128,48,128]{3,2,1,0:T(8,128)(2,1)} %param.11) | copy-start | bytes 4718596
  3.6 23.0 %all-to-all-start = ((bf16[16,1,2,128,128]{4,3,2,1,0:T(8,128)(2,1)}), bf16[16,1,2,128,128]{4,3,2,1,0:T(8,128)(2,1)}, u32[]{:S(2)}, u32[]{:S(2)}) async-start(bf16[16,1,2,128,128]{4,3,2,1,0:T(8,128)(2,1)} %maximum_bitcast_fusion.3), calls=%async_computation | async-start | bytes 2097152 | tf_op jit(solution)/shard_map/all_to_all | solution.py:205
  10.9 2.1 %copy-start.9 = (s32[1,16,12]{1,0,2:T(1,128)S(1)}, s32[1,16,12]{1,0,2:T(1,128)}, u32[]{:S(2)}) copy-start(s32[1,16,12]{1,0,2:T(1,128)} %param.13) | copy-start | bytes 2308
  26.6 31.4 %all-to-all-start.1 = ((bf16[16,2,2,128,128]{4,3,2,1,0:T(8,128)(2,1)}), bf16[16,2,2,128,128]{4,3,2,1,0:T(8,128)(2,1)S(1)}, u32[]{:S(2)}, u32[]{:S(2)}) async-start(bf16[16,2,2,128,128]{4,3,2,1,0:T(8,128)(2,1)} %pad_maximum_fusion.1), calls=%async_computation.1 | async-start | bytes 4194304 | tf_op jit(solution)/shard_map/all_to_all | solution.py:205
  39.5 1.9 copy-start.6
  41.4 1.4 copy-start.5
  58.0 99.8 %all-to-all-start.2 = ((bf16[16,3,3,128,128]{4,3,2,1,0:T(8,128)(2,1)}), bf16[16,3,3,128,128]{4,3,2,1,0:T(8,128)(2,1)}, u32[]{:S(2)}, u32[]{:S(2)}) async-start(bf16[16,3,3,128,128]{4,3,2,1,0:T(8,128)(2,1)} %pad_maximum_fusion), calls=%async_computation.2 | async-start | bytes 9437184 | tf_op jit(solution)/shard_map/all_to_all | solution.py:205
  64.5 22.1 %collective-permute-start = (bf16[16,1,2,128,128]{4,3,2,1,0:T(8,128)(2,1)}, bf16[16,1,2,128,128]{4,3,2,1,0:T(8,128)(2,1)S(1)}, u32[]{:S(2)}, u32[]{:S(2)}) collective-permute-start(bf16[16,1,2,128,128]{4,3,2,1,0:T(8,128)(2,1)} %all-to-all-done), channel_id=1, source_target_pairs={{0,16},{16,32},{32,48},{48,64},{64,80},{80,96},{96,112},{112,128},... | collective-permute-start | bytes 3145736 | tf_op jit(solution)/shard_map/ppermute | solution.py:210
  71.8 37.1 %collective-permute-start.6 = (bf16[16,1,2,128,128]{4,3,2,1,0:T(8,128)(2,1)S(1)}, bf16[16,1,2,128,128]{4,3,2,1,0:T(8,128)(2,1)S(1)}, u32[]{:S(2)}, u32[]{:S(2)}) collective-permute-start(bf16[16,1,2,128,128]{4,3,2,1,0:T(8,128)(2,1)S(1)} %get-tuple-element.29), channel_id=1, source_target_pairs={{0,16},{16,32},{32,48},{48,64},{64,80},{80,96},{96,112},{112,128},... | collective-permute-start | bytes 3145736 | tf_op jit(solution)/shard_map/ppermute | solution.py:210
  73.7 54.8 %collective-permute-start.3 = (bf16[16,1,2,128,128]{4,3,2,1,0:T(8,128)(2,1)S(1)}, bf16[16,1,2,128,128]{4,3,2,1,0:T(8,128)(2,1)}, u32[]{:S(2)}, u32[]{:S(2)}) collective-permute-start(bf16[16,1,2,128,128]{4,3,2,1,0:T(8,128)(2,1)S(1)} %get-tuple-element.30), channel_id=1, source_target_pairs={{0,16},{16,32},{32,48},{48,64},{64,80},{80,96},{96,112},{112,128},... | collective-permute-start | bytes 3145736 | tf_op jit(solution)/shard_map/ppermute | solution.py:210
  76.7 57.5 %collective-permute-start.2 = (bf16[16,1,2,128,128]{4,3,2,1,0:T(8,128)(2,1)}, bf16[16,1,2,128,128]{4,3,2,1,0:T(8,128)(2,1)S(1)}, u32[]{:S(2)}, u32[]{:S(2)}) collective-permute-start(bf16[16,1,2,128,128]{4,3,2,1,0:T(8,128)(2,1)} %all-to-all-done), channel_id=1, source_target_pairs={{0,48},{32,80},{64,112},{96,144},{128,176},{160,208},{192,240},{1,... | collective-permute-start | bytes 3145736 | tf_op jit(solution)/shard_map/ppermute | solution.py:214
  86.5 48.7 %collective-permute-start.1 = (bf16[16,1,2,128,128]{4,3,2,1,0:T(8,128)(2,1)S(1)}, bf16[16,1,2,128,128]{4,3,2,1,0:T(8,128)(2,1)}, u32[]{:S(2)}, u32[]{:S(2)}) collective-permute-start(bf16[16,1,2,128,128]{4,3,2,1,0:T(8,128)(2,1)S(1)} %collective-permute-done.refs_2_), channel_id=1, source_target_pairs={{0,32},{32,64},{64,96},{96,128},{128,160},{160,192},{192,224},{1,3... | collective-permute-start | bytes 3145736 | tf_op jit(solution)/shard_map/ppermute | solution.py:214
  108.9 30.8 %collective-permute-start.7 = (bf16[16,1,2,128,128]{4,3,2,1,0:T(8,128)(2,1)S(1)}, bf16[16,1,2,128,128]{4,3,2,1,0:T(8,128)(2,1)}, u32[]{:S(2)}, u32[]{:S(2)}) collective-permute-start(bf16[16,1,2,128,128]{4,3,2,1,0:T(8,128)(2,1)S(1)} %collective-permute-done.6.refs_6_), channel_id=1, source_target_pairs={{0,16},{16,32},{32,48},{48,64},{64,80},{80,96},{96,112},{112,128},... | collective-permute-start | bytes 3145736 | tf_op jit(solution)/shard_map/ppermute | solution.py:210
  128.5 22.6 %collective-permute-start.4 = (bf16[16,1,2,128,128]{4,3,2,1,0:T(8,128)(2,1)}, bf16[16,1,2,128,128]{4,3,2,1,0:T(8,128)(2,1)}, u32[]{:S(2)}, u32[]{:S(2)}) collective-permute-start(bf16[16,1,2,128,128]{4,3,2,1,0:T(8,128)(2,1)} %collective-permute-done.3.refs_4_), channel_id=1, source_target_pairs={{0,16},{16,32},{32,48},{48,64},{64,80},{80,96},{96,112},{112,128},... | collective-permute-start | bytes 3145736 | tf_op jit(solution)/shard_map/ppermute | solution.py:210
  134.2 23.6 %copy-start.4 = (s32[1,16]{1,0:T(1,128)S(1)}, s32[1,16]{1,0:T(1,128)}, u32[]{:S(2)}) copy-start(s32[1,16]{1,0:T(1,128)} %param.14) | copy-start | bytes 196
  134.2 1.0 copy-start.8
  136.6 20.2 %collective-permute-start.9 = (bf16[16,1,2,128,128]{4,3,2,1,0:T(8,128)(2,1)S(1)}, bf16[16,1,2,128,128]{4,3,2,1,0:T(8,128)(2,1)S(1)}, u32[]{:S(2)}, u32[]{:S(2)}) collective-permute-start(bf16[16,1,2,128,128]{4,3,2,1,0:T(8,128)(2,1)S(1)} %get-tuple-element.44), channel_id=1, source_target_pairs={{0,16},{32,48},{64,80},{96,112},{128,144},{160,176},{192,208},{224... | collective-permute-start | bytes 3145736 | tf_op jit(solution)/shard_map/ppermute | solution.py:214
  139.7 36.2 %collective-permute-start.8 = (bf16[16,1,2,128,128]{4,3,2,1,0:T(8,128)(2,1)}, bf16[16,1,2,128,128]{4,3,2,1,0:T(8,128)(2,1)}, u32[]{:S(2)}, u32[]{:S(2)}) collective-permute-start(bf16[16,1,2,128,128]{4,3,2,1,0:T(8,128)(2,1)} %collective-permute-done.7.refs_5_), channel_id=1, source_target_pairs={{0,16},{16,32},{32,48},{48,64},{64,80},{80,96},{96,112},{112,128},... | collective-permute-start | bytes 3145736 | tf_op jit(solution)/shard_map/ppermute | solution.py:210
  151.1 24.9 %collective-permute-start.5 = (bf16[16,1,2,128,128]{4,3,2,1,0:T(8,128)(2,1)}, bf16[16,1,2,128,128]{4,3,2,1,0:T(8,128)(2,1)}, u32[]{:S(2)}, u32[]{:S(2)}) collective-permute-start(bf16[16,1,2,128,128]{4,3,2,1,0:T(8,128)(2,1)} %collective-permute-done.4.refs_3_), channel_id=1, source_target_pairs={{0,16},{16,32},{32,48},{48,64},{64,80},{80,96},{96,112},{112,128},... | collective-permute-start | bytes 3145736 | tf_op jit(solution)/shard_map/ppermute | solution.py:210
  156.9 1.0 copy-start.2
  157.8 1.2 copy-start.3
  212.2 1.7 copy-start.1
